TPU v7x, 256 devices: a whole 4x4x8 slice. The times are simulated.
256 devices in a mesh: band: 8 (over y_hi, x), item: 32 (over y_lo, z, core).
Axes of the slice: x: 4, y: 4 (y_hi: 2, y_lo: 2; y = y_hi * 2 + y_lo), z: 8, core: 2. Of those that a mesh axis runs over, the one named last changes fastest.
Arguments:
- ratings: bfloat16 [49152, 16384], P('band', 'item'), may hold values from -6 to 6
- rating_mask: int32 [384, 16384], P('band', 'item'), may hold values 0 or 1
- attributes: bfloat16 [24576, 16384], P('band', 'item'), may hold values from -6 to 6
- attribute_mask: int32 [192, 16384], P('band', 'item'), may hold values 0 or 1
- user_factors: bfloat16 [49152, 256], P('band', 'item'), as said below
- tag_factors: bfloat16 [24576, 256], P('band', 'item'), as said below
Outputs:
- item_factors: float32 [16384, 256], P('item')
Inputs may be any that keep to these rules, and one draw needn't show every extreme that they name: `user_factors`: user factors of order one over the square root of 49152. `tag_factors`: tag factors of order one over the square root of 24576.
All inputs are finite; a program needn't handle non-finite values. No bound on the sum of `rating_mask` or of `attribute_mask` on one device may be relied on, other than what follows from the above.
Results may differ from a plain program's by a relative error of at most 0.0003.
Values may be sent and summed in bfloat16 or wider, within the bound.
No kernel may reach another device: no remote copies, remote signals or barrier semaphores. Data moves between devices by JAX's collectives and lax.ppermute only.
A program may use at most 64 MiB of HBM per device.

v0:
```python
import jax
import jax.numpy as jnp
from jax import lax
from jax.sharding import PartitionSpec as P

LAMBDA = 0.5
REG = 0.1


def apply_mask(values, mask):
    rows, cols = values.shape
    blocks = mask.shape[0]
    shaped = values.reshape(blocks, rows // blocks, cols) * mask.astype(values.dtype)[:, None, :]
    return shaped.reshape(rows, cols)


def inner(left, right):
    return lax.dot_general(
        left, right, (((0,), (0,)), ((), ())), preferred_element_type=jnp.float32
    )


def solve_rows(factor, rhs):
    half = lax.linalg.triangular_solve(factor, rhs, left_side=False, lower=True, transpose_a=True)
    return lax.linalg.triangular_solve(factor, half, left_side=False, lower=True, transpose_a=False)


def band_gram(partial_gram):
    return lax.psum(partial_gram, "band")


def finish_gram(summed_gram, rank):
    return jnp.linalg.cholesky(summed_gram + REG * jnp.eye(rank, dtype=jnp.float32))


def body(ratings, rating_mask, attributes, attribute_mask, user_factors, tag_factors):
    users = lax.all_gather(user_factors, "item", axis=1, tiled=True)
    tags = lax.all_gather(tag_factors, "item", axis=1, tiled=True)
    rank = users.shape[1]
    partial_gram = inner(users, users) + LAMBDA * inner(tags, tags)
    masked_ratings = apply_mask(ratings, rating_mask)
    masked_attributes = apply_mask(attributes, attribute_mask)
    local_rhs = inner(masked_ratings, users) + LAMBDA * inner(masked_attributes, tags)
    summed_gram = band_gram(partial_gram)
    summed_rhs = lax.psum(local_rhs, "band")
    factor = finish_gram(summed_gram, rank)
    return solve_rows(factor, summed_rhs)


def solution(mesh):
    in_specs = (
        P("band", "item"),
        P("band", "item"),
        P("band", "item"),
        P("band", "item"),
        P("band", "item"),
        P("band", "item"),
    )
    out_specs = P("item", None)
    return jax.shard_map(body, mesh=mesh, in_specs=in_specs, out_specs=out_specs, check_vma=False)
```

profile of v0, /device:TPU:1, one launch (start us, length us, event | category | flops | bytes accessed | tf_op | source)
XLA Modules:
  0.0 312.8 jit_solution(6339761031712931756)
XLA Ops:
  6.5 0.0 all-gather.5.cloned.1.call-start
  6.5 0.7 all-gather.5.cloned.1.call-update
  7.3 0.0 all-gather.3.cloned.1.call-start
  7.3 0.7 all-gather.3.cloned.1.call-update
  8.0 0.0 all-reduce.4.cloned.1.call-start
  8.1 0.8 convert_element_type.8
  8.9 0.9 convert_element_type.7
  9.8 0.0 copy-start
  9.8 2.3 bitcast_multiply_fusion.1
  12.0 1.5 copy-done
  13.5 3.1 bitcast_multiply_fusion
  16.6 61.2 %all-gather.5.cloned.1.call-done = bf16[3072,256]{0,1:T(8,128)(2,1)} async-done(((bf16[3072,8]{0,1:T(8,128)(2,1)}), bf16[3072,256]{0,1:T(8,128)(2,1)}) %all-gather.5.cloned.1.call-update) | async-done | bytes 1572880 | tf_op jit(solution)/shard_map/all_gather | solution.py:38
  77.8 3.2 %convolution_multiply_fusion = f32[512,256]{1,0:T(8,128)} fusion(bf16[3072,512]{1,0:T(8,128)(2,1)S(1)} %bitcast_multiply_fusion.1, bf16[3072,256]{0,1:T(8,128)(2,1)} %all-gather.5.cloned.1.call-done), kind=kOutput, calls=%fused_computation.4 | convolution fusion | flops 805437440 | bytes 5242880 | tf_op jit(solution)/shard_map/dot_general | solution.py:18
  81.0 0.0 copy-start.2
  81.0 64.4 %all-gather.3.cloned.1.call-done = bf16[6144,256]{0,1:T(8,128)(2,1)} async-done(((bf16[6144,8]{0,1:T(8,128)(2,1)}), bf16[6144,256]{0,1:T(8,128)(2,1)}) %all-gather.3.cloned.1.call-update) | async-done | bytes 3145744 | tf_op jit(solution)/shard_map/all_gather | solution.py:37
  145.4 4.0 %fusion.13 = f32[256,256]{1,0:T(8,128)S(1)} fusion(bf16[6144,256]{0,1:T(8,128)(2,1)} %all-gather.3.cloned.1.call-done), kind=kOutput, calls=%fused_computation.41 | convolution fusion | flops 805306368 | bytes 3407872 | tf_op jit(solution)/shard_map/dot_general | solution.py:18
  149.4 0.0 copy-done.2
  149.4 0.0 copy-start.4
  149.5 1.3 fusion
  150.7 0.0 copy-done.1
  150.8 0.0 copy-done.4
  150.8 4.5 %convolution_add_fusion = f32[512,256]{1,0:T(8,128)} fusion(f32[512,256]{1,0:T(8,128)S(1)} %copy-done.4, bf16[6144,512]{1,0:T(8,128)(2,1)S(1)} %copy-done.1, bf16[6144,256]{0,1:T(8,128)(2,1)} %all-gather.3.cloned.1.call-done), kind=kOutput, calls=%fused_computation.5 | convolution fusion | flops 1610743808 | bytes 10485760 | tf_op jit(solution)/shard_map/dot_general | solution.py:18
  155.3 0.0 all-reduce.4.cloned.1.call-update
  155.3 85.5 %all-reduce.4.cloned.1.call-done = (f32[512,256]{1,0:T(8,128)}, f32[256,256]{1,0:T(8,128)}) async-done(((f32[512,256]{1,0:T(8,128)}, f32[256,256]{1,0:T(8,128)}), (f32[512,256]{1,0:T(8,128)}, f32[256,256]{1,0:T(8,128)})) %all-reduce.4.cloned.1.call-update) | async-done | bytes 786448 | tf_op jit(solution)/shard_map/psum | solution.py:45
  240.8 1.0 select_add_fusion
  241.9 0.1 copy.7
  242.0 1.0 fusion.3
  243.0 11.7 %cholesky.49 = f32[128,128]{1,0:T(8,128)S(1)} custom-call(f32[128,128]{1,0:T(8,128)S(1)} %cholesky.115), custom_call_target="Cholesky" | custom-call | tf_op jit(solution)/shard_map/jit(cholesky)/cholesky | solution.py:33
  254.8 9.8 %custom-call.16 = f32[1,128,128]{1,2,0:T(8,128)S(1)} custom-call(f32[1,128,128]{2,1,0:T(8,128)S(1)} %get-tuple-element.28), custom_call_target="InvertDiagBlocksLowerTriangular" | custom-call | tf_op jit(solution)/shard_map/jit(cholesky)/cholesky | solution.py:33
  264.6 0.2 constant_dynamic-update-slice_fusion.1
  264.8 0.3 convolution_subtract_fusion.2
  265.1 11.9 %cholesky.103 = f32[128,128]{1,0:T(8,128)S(1)} custom-call(f32[128,128]{1,0:T(8,128)S(1)} %convolution_subtract_fusion.2), custom_call_target="Cholesky" | custom-call | tf_op jit(solution)/shard_map/jit(cholesky)/cholesky | solution.py:33
  277.0 0.7 compare_reduce_fusion
  279.0 0.1 triangular_solve.70
  279.0 3.9 %while.1 = (s32[]{:T(128)}, f32[256,256]{1,0:T(8,128)S(1)}, s32[2,2]{1,0:T(2,128)S(1)}, f32[2,128,128]{2,1,0:T(8,128)S(1)}, s32[]{:T(128)}) while((s32[]{:T(128)}, f32[256,256]{1,0:T(8,128)S(1)}, s32[2,2]{1,0:T(2,128)S(1)}, f32[2,128,128]{2,1,0:T(8,128)S(1)}, s32[]{:T(128)}) %tuple.23), condition=%wide.while_cond, body=%wide.while_body.sunk | while | flops 2 | bytes 131189 | solution.py:24
  279.1 0.6 fusion.30
  279.6 1.4 bitcast_dynamic-update-slice_fusion.2
  281.0 0.6 fusion.30
  281.6 1.4 bitcast_dynamic-update-slice_fusion.2
  283.0 19.7 %custom-call.17 = f32[2,128,128]{1,2,0:T(8,128)S(1)} custom-call(f32[2,128,128]{2,1,0:T(8,128)S(1)} %get-tuple-element.12), custom_call_target="InvertDiagBlocksLowerTriangular" | custom-call | tf_op jit(solution)/shard_map/triangular_solve | solution.py:24
  302.7 0.0 copy-done.3
  302.7 0.4 fusion.1
  303.0 0.4 convolution_subtract_fusion.1
  303.4 0.4 fusion.9
  303.8 0.4 fusion.8
  304.2 0.6 convolution_subtract_fusion
  304.8 0.4 fusion.7
  305.2 1.0 copy.8
  (12 shorter events, 0.2 us)
Async XLA Ops:
  6.5 71.2 %all-gather.5.cloned.1.call-start = ((), (), s32[]{:S(2)}) async-start(), calls=%async_computation.1 | async-start | bytes 1622016 | tf_op jit(solution)/shard_map/all_gather | solution.py:38
  7.3 138.2 %all-gather.3.cloned.1.call-start = ((), (), s32[]{:S(2)}) async-start(), calls=%async_computation | async-start | bytes 3244032 | tf_op jit(solution)/shard_map/all_gather | solution.py:37
  8.0 232.8 %all-reduce.4.cloned.1.call-start = ((), (), s32[]{:S(2)}) async-start(), calls=%async_computation.2 | async-start | bytes 1572864 | tf_op jit(solution)/shard_map/psum | solution.py:45
  9.8 3.7 %copy-start = (bf16[6144,512]{1,0:T(8,128)(2,1)S(1)}, bf16[6144,512]{1,0:T(8,128)(2,1)}, u32[]{:S(2)}) copy-start(bf16[6144,512]{1,0:T(8,128)(2,1)} %param.6) | copy-start | bytes 18874372
  81.0 68.4 %copy-start.2 = (bf16[3072,256]{0,1:T(8,128)(2,1)S(1)}, bf16[3072,256]{0,1:T(8,128)(2,1)}, u32[]{:S(2)}) copy-start(bf16[3072,256]{0,1:T(8,128)(2,1)} %all-gather.5.cloned.1.call-done) | copy-start | bytes 4718596
  145.4 5.3 %copy-start.1 = (bf16[6144,512]{1,0:T(8,128)(2,1)S(1)}, bf16[6144,512]{1,0:T(8,128)(2,1)}, u32[]{:S(2)}) copy-start(bf16[6144,512]{1,0:T(8,128)(2,1)} %bitcast_multiply_fusion) | copy-start | bytes 18874372
  149.4 1.3 copy-start.4
  240.8 61.8 %copy-start.3 = (f32[512,256]{1,0:T(8,128)S(1)}, f32[512,256]{1,0:T(8,128)}, u32[]{:S(2)}) copy-start(f32[512,256]{1,0:T(8,128)} %get-tuple-element.21) | copy-start | bytes 1572868
Sparse Core Ops, SparseCore 0:
  9.2 68.5 all-gather.4
  79.6 65.7 all-gather.2
  155.4 85.3 all-reduce.3
where the time goes:
time: 317 us; the launch traced here: 313 us
  waiting for transfers between devices  213 us (67%)
  other arithmetic  63 us (20%)
  matrix products  16 us (5%)
  between operations  14.6 us (5%)
  local copies, waits for them, and re-layouts  6.6 us (2%)
    psum x1, waiting for transfers between devices, body(): summed_rhs = lax.psum(local_rhs, 'band')  85.5 us
    all_gather x1, waiting for transfers between devices, body(): users = lax.all_gather(user_factors, 'item', axis=1, tiled=True)  64.4 us
    all_gather x1, waiting for transfers between devices, body(): tags = lax.all_gather(tag_factors, 'item', axis=1, tiled=True)  61.2 us
    another operation x6, other arithmetic, finish_gram(): jnp.linalg.cholesky(summed_gram + REG * jnp.eye(rank, dtype=jnp.float32))  34.1 us
    another operation x3, other arithmetic, solve_rows(): lax.linalg.triangular_solve(factor, rhs, left_side=False, lower=True, tra...  19.7 us
    dot_general x4, matrix products, inner(): lax.dot_general(left, right, (((0,), (0,)), ((), ())), preferred_element_...  13 us
  transfers between devices with their start and end apart: 3, of which 3 were waited for; matrix products, arithmetic and copies ran while one was open for 3% of the time, Pallas kernels for 0%

commit v1 on v0

v1 whole, which is shorter than its diff:
```python
import functools

import jax
import jax.numpy as jnp
from jax import lax
from jax.experimental import pallas as pl
from jax.experimental.pallas import tpu as pltpu
from jax.sharding import PartitionSpec as P

LAMBDA = 0.5
REG = 0.1
STEP = 1024
PANEL = 8

NY, NZ, NC = 2, 8, 2
NYH, NX = 2, 4
NT = (((1,), (1,)), ((), ()))


def item_of(y, z, c):
    return ((y % NY) * NZ + z % NZ) * NC + c % NC


def item_perm(dy, dz, dc):
    places = [(y, z, c) for y in range(NY) for z in range(NZ) for c in range(NC)]
    return [(item_of(y, z, c), item_of(y + dy, z + dz, c + dc)) for y, z, c in places]


def band_perm(stage):
    pairs = []
    for yh in range(NYH):
        for x in range(NX):
            for item in range(NY * NZ * NC):
                if stage == 2:
                    to = (1 - yh) * NX + x
                elif stage == item % NC:
                    to = yh * NX + (x ^ 1)
                else:
                    to = yh * NX + (NX - 1 - x)
                pairs.append(((yh * NX + x) * 32 + item, to * 32 + item))
    return pairs


UP = item_perm(0, 1, 0)
DOWN = item_perm(0, -1, 0)
ACROSS = item_perm(1, 0, 0)
CORE = item_perm(0, 0, 1)
OFFSETS = (0, -1, 1, -2, 2, -3, 3, 4)


def gather_columns(own):
    half = own.shape[1] // 2
    up = down = own
    near = [own]
    far = [lax.ppermute(own, "item", ACROSS)]
    for step in range(1, 4):
        up = lax.ppermute(up, "item", UP)
        down = lax.ppermute(down, "item", DOWN)
        both = jnp.concatenate([up, down], axis=0)
        near.append(both)
        far.append(lax.ppermute(both, "item", ACROSS))
    last = jnp.concatenate(
        [lax.ppermute(up[:, :half], "item", UP), lax.ppermute(down[:, half:], "item", DOWN)], axis=1
    )
    near.append(last)
    far.append(lax.ppermute(last, "item", ACROSS))
    return jnp.concatenate(near + far, axis=0)


def gram_kernel(users, mine_ref, other_ref, out_ref):
    step = pl.program_id(0)

    @pl.when(step == 0)
    def _():
        out_ref[...] = jnp.zeros_like(out_ref)

    scale = jnp.where(step < users, 1.0, LAMBDA).astype(jnp.bfloat16)
    mine = mine_ref[...]
    scaled = mine * scale
    out_ref[:, :128] += lax.dot_general(scaled, mine, NT, preferred_element_type=jnp.float32)
    out_ref[:, 128:] += lax.dot_general(scaled, other_ref[...], NT, preferred_element_type=jnp.float32)


def top_gram(mine, other, n_users):
    rows = mine.shape[1]
    spec = pl.BlockSpec((128, STEP), lambda i: (0, i))
    return pl.pallas_call(
        functools.partial(gram_kernel, n_users // STEP),
        out_shape=jax.ShapeDtypeStruct((128, 256), jnp.float32),
        grid=(rows // STEP,),
        in_specs=[spec, spec],
        out_specs=pl.BlockSpec((128, 256), lambda i: (0, 0)),
        name="top_gram",
    )(mine, other)


def rhs_kernel(users, mine_ref, other_ref, rate_ref, rate_mask_ref, attr_ref, attr_mask_ref, out_ref):
    step = pl.program_id(0)

    @pl.when(step == 0)
    def _():
        out_ref[...] = jnp.zeros_like(out_ref)

    def add(value_ref, mask_ref, scale):
        parts = []
        for block in range(STEP // 128):
            keep = mask_ref[0, block : block + 1, :].astype(jnp.float32) * scale
            parts.append(value_ref[block * 128 : (block + 1) * 128, :] * keep.astype(jnp.bfloat16))
        masked = jnp.concatenate(parts, axis=0)
        out_ref[:128, :] += jnp.dot(mine_ref[...], masked, preferred_element_type=jnp.float32)
        out_ref[128:, :] += jnp.dot(other_ref[...], masked, preferred_element_type=jnp.float32)

    @pl.when(step < users)
    def _():
        add(rate_ref, rate_mask_ref, 1.0)

    @pl.when(step >= users)
    def _():
        add(attr_ref, attr_mask_ref, LAMBDA)


def rhs_rows(mine, other, ratings, rating_mask, attributes, attribute_mask):
    users = ratings.shape[0] // STEP
    tags = attributes.shape[0] // STEP
    items = ratings.shape[1]
    blocks = STEP // 128
    factor = pl.BlockSpec((128, STEP), lambda i: (0, i))
    first = lambda i: jnp.minimum(i, users - 1)
    second = lambda i: jnp.maximum(i - users, 0)
    return pl.pallas_call(
        functools.partial(rhs_kernel, users),
        out_shape=jax.ShapeDtypeStruct((256, items), jnp.float32),
        grid=(users + tags,),
        in_specs=[
            factor,
            factor,
            pl.BlockSpec((STEP, items), lambda i: (first(i), 0)),
            pl.BlockSpec((1, blocks, items), lambda i: (first(i), 0, 0)),
            pl.BlockSpec((STEP, items), lambda i: (second(i), 0)),
            pl.BlockSpec((1, blocks, items), lambda i: (second(i), 0, 0)),
        ],
        out_specs=pl.BlockSpec((256, items), lambda i: (0, 0)),
        compiler_params=pltpu.CompilerParams(vmem_limit_bytes=48 << 20),
        name="rhs_rows",
    )(
        mine,
        other,
        ratings,
        rating_mask.reshape(users, blocks, items),
        attributes,
        attribute_mask.reshape(tags, blocks, items),
    )


def inverse_kernel(order_ref, top_ref, peer_ref, out_ref, a_ref):
    n = a_ref.shape[0]
    h = n // 2
    a_ref[:h, :] = top_ref[...]
    a_ref[h:, :h] = peer_ref[:, h:]
    a_ref[h:, h:] = peer_ref[:, :h]
    rows = lax.broadcasted_iota(jnp.int32, (n, n), 0)
    cols = lax.broadcasted_iota(jnp.int32, (n, n), 1)
    a_ref[...] = a_ref[...] + jnp.where(rows == cols, REG, 0.0)
    sub = lax.broadcasted_iota(jnp.int32, (PANEL, n), 0)
    lane = lax.broadcasted_iota(jnp.int32, (PANEL, n), 1)

    for p in range(n // PANEL):
        r0 = p * PANEL
        panel = a_ref[r0 : r0 + PANEL, :]
        before = panel
        for j in range(PANEL):
            k = r0 + j
            column = panel[:, k : k + 1]
            inv = 1.0 / panel[j : j + 1, k : k + 1]
            row = jnp.where(lane[:1] == k, inv, panel[j : j + 1, :] * inv)
            rest = jnp.where(lane == k, 0.0, panel) - column * row
            panel = jnp.where(sub == j, row, rest)
        inside = (rows >= r0) & (rows < r0 + PANEL)
        here = (cols >= r0) & (cols < r0 + PANEL)
        left = a_ref[:, r0 : r0 + PANEL]
        change = jnp.dot(left, panel, preferred_element_type=jnp.float32, precision=lax.Precision.HIGHEST)
        a = jnp.where(here, 0.0, a_ref[...]) - change
        a_ref[...] = a
        a_ref[r0 : r0 + PANEL, :] = panel

    for b in range(n // 8):
        out_ref[pl.ds(pl.multiple_of(order_ref[b] * 8, 8), 8), :] = a_ref[b * 8 : (b + 1) * 8, :]


def ordered_inverse(order, top, peer):
    n = top.shape[1]
    return pl.pallas_call(
        inverse_kernel,
        out_shape=jax.ShapeDtypeStruct((n, n), jnp.float32),
        grid_spec=pltpu.PrefetchScalarGridSpec(
            num_scalar_prefetch=1,
            grid=(1,),
            in_specs=[pl.BlockSpec(top.shape, lambda i, o: (0, 0)), pl.BlockSpec(top.shape, lambda i, o: (0, 0))],
            out_specs=pl.BlockSpec((n, n), lambda i, o: (0, 0)),
            scratch_shapes=[pltpu.VMEM((n, n), jnp.float32)],
        ),
        name="ordered_inverse",
    )(order, top, peer)


def final_kernel(rhs_ref, more_ref, inverse_ref, out_ref):
    rhs = rhs_ref[...] + more_ref[...]
    out_ref[...] = lax.dot_general(
        rhs,
        inverse_ref[...],
        (((0,), (1,)), ((), ())),
        preferred_element_type=jnp.float32,
        precision=lax.Precision.HIGHEST,
    )


def final_solve(rhs, more, inverse):
    k, items = rhs.shape
    return pl.pallas_call(
        final_kernel,
        out_shape=jax.ShapeDtypeStruct((items, k), jnp.float32),
        name="final_solve",
    )(rhs, more, inverse)


def both(value, stage):
    return value + lax.ppermute(value, ("band", "item"), band_perm(stage))


def body(ratings, rating_mask, attributes, attribute_mask, user_factors, tag_factors):
    n_users = user_factors.shape[0]
    own = jnp.concatenate([user_factors.T, tag_factors.T], axis=1)
    mine = gather_columns(own)
    other = lax.ppermute(mine, "item", CORE)

    item = lax.axis_index("item")
    y, z, c = item // (NZ * NC), (item // NC) % NZ, item % NC
    order = []
    for dc in range(2):
        for dy in range(2):
            for dz in OFFSETS:
                order.append((((y + dy) % NY) * NZ + (z + dz) % NZ) * NC + (c + dc) % NC)
    order = jnp.stack(order).astype(jnp.int32)

    top = top_gram(mine, other, n_users)
    rhs = rhs_rows(mine, other, ratings, rating_mask, attributes, attribute_mask)
    for stage in range(3):
        top = both(top, stage)
    peer = lax.ppermute(top, "item", CORE)
    inverse = ordered_inverse(order, top, peer)
    for stage in range(2):
        rhs = both(rhs, stage)
    more = lax.ppermute(rhs, ("band", "item"), band_perm(2))
    return final_solve(rhs, more, inverse)


def solution(mesh):
    spec = P("band", "item")
    return jax.shard_map(
        body, mesh=mesh, in_specs=(spec,) * 6, out_specs=P("item", None), check_vma=False
    )
```

time: 317 us -> 138 us (0.44); the launches traced: 313 us -> 137 us
  waiting for transfers between devices: 213 us -> 34.1 us
  other arithmetic: 63 us -> 2.13 us
  Pallas kernels: 0 us -> 57.8 us
  starting transfers between devices: 0.08 us -> 40.7 us
  matrix products: 16 us -> 0 us
  between operations: 14.6 us -> 0.23 us
  local copies, waits for them, and re-layouts: 6.6 us -> 2.37 us
    all_gather x2 -> x0, waiting for transfers between devices: 126 us -> none  [the longest x1 64.4 us: body(): users = lax.all_gather(user_factors, 'item', axis=1, tiled=True)]
    psum x1 -> x0, waiting for transfers between devices: 85.5 us -> none  [body(): summed_rhs = lax.psum(local_rhs, 'band')]
    pallas_call x0 -> x4, Pallas kernels: none -> 57.8 us  [the longest x1 38.1 us: ordered_inverse(): pl.pallas_call(inverse_kernel, out_shape=jax.ShapeDtypeStruct((n, n), jnp...]
    another operation x10 -> x0, other arithmetic: 53.9 us -> none  [the longest x6 34.1 us: finish_gram(): jnp.linalg.cholesky(summed_gram + REG * jnp.eye(rank, dtype=jnp.float32))]
    ppermute x0 -> x21, starting transfers between devices: none -> 40.7 us  [the longest x5 9.03 us: both(): return value + lax.ppermute(value, ('band', 'item'), band_perm(stage))]
    ppermute x0 -> x21, waiting for transfers between devices: none -> 34.1 us  [the longest x5 15.8 us: both(): return value + lax.ppermute(value, ('band', 'item'), band_perm(stage))]
    dot_general x4 -> x0, matrix products: 13 us -> none  [inner(): lax.dot_general(left, right, (((0,), (0,)), ((), ())), preferred_element_...]
    mul x2 -> x0, other arithmetic: 5.35 us -> none  [apply_mask(): values.reshape(blocks, rows // blocks, cols)]
  transfers between devices with their start and end apart: 3 -> 21, of which waited for: 3 -> 12; matrix products, arithmetic and copies ran while one was open for 3% -> 1% of each run, Pallas kernels for 0% -> 33%
where the time goes in v1:
time: 138 us; the launch traced here: 137 us
  Pallas kernels  57.8 us (42%)
  starting transfers between devices  40.7 us (29%)
  waiting for transfers between devices  34.1 us (25%)
  local copies, waits for them, and re-layouts  2.37 us (2%)
  other arithmetic  2.13 us (2%)
    pallas_call x1, Pallas kernels, ordered_inverse(): pl.pallas_call(inverse_kernel, out_shape=jax.ShapeDtypeStruct((n, n), jnp...  38.1 us
    ppermute x5, waiting for transfers between devices, both(): return value + lax.ppermute(value, ('band', 'item'), band_perm(stage))  15.8 us
    pallas_call x1, Pallas kernels, rhs_rows(): pl.pallas_call(functools.partial(rhs_kernel, users), out_shape=jax.ShapeD...  9.53 us
    ppermute x5, starting transfers between devices, both(): return value + lax.ppermute(value, ('band', 'item'), band_perm(stage))  9.03 us
    ppermute x3, starting transfers between devices, gather_columns(): down = lax.ppermute(down, 'item', DOWN)  7.55 us
    pallas_call x1, Pallas kernels, top_gram(): pl.pallas_call(functools.partial(gram_kernel, n_users // STEP), out_shape...  7.42 us
    ppermute x3, waiting for transfers between devices, gather_columns(): up = lax.ppermute(up, 'item', UP)  7.14 us
    ppermute x1, starting transfers between devices, body(): other = lax.ppermute(mine, 'item', CORE)  6.47 us
  transfers between devices with their start and end apart: 21, of which 12 were waited for; matrix products, arithmetic and copies ran while one was open for 1% of the time, Pallas kernels for 33%

profile of v1, /device:TPU:1, one launch (start us, length us, event | category | flops | bytes accessed | tf_op | source)
XLA Modules:
  0.0 137.3 jit_solution(11325942251897479140)
XLA Ops:
  0.0 0.9 pad_maximum_fusion.4
  0.9 2.5 %collective-permute-start = (bf16[8,9216]{1,0:T(8,128)(2,1)S(1)}, bf16[8,9216]{1,0:T(8,128)(2,1)S(1)}, u32[]{:S(2)}, u32[]{:S(2)}) collective-permute-start(bf16[8,9216]{1,0:T(8,128)(2,1)S(1)} %get-tuple-element.5), channel_id=1, source_target_pairs={{0,2},{1,3},{2,4},{3,5},{4,6},{5,7},{6,8},{7,9},{8,10},{9,11},{10,... | collective-permute-start | bytes 442376 | tf_op jit(solution)/shard_map/ppermute | solution.py:57
  3.5 4.0 %collective-permute-start.1 = (bf16[8,9216]{1,0:T(8,128)(2,1)S(1)}, bf16[8,9216]{1,0:T(8,128)(2,1)S(1)}, u32[]{:S(2)}, u32[]{:S(2)}) collective-permute-start(bf16[8,9216]{1,0:T(8,128)(2,1)S(1)} %get-tuple-element.5), channel_id=1, source_target_pairs={{0,14},{1,15},{2,0},{3,1},{4,2},{5,3},{6,4},{7,5},{8,6},{9,7},{10,... | collective-permute-start | bytes 442376 | tf_op jit(solution)/shard_map/ppermute | solution.py:58
  7.5 1.3 collective-permute-start.8
  8.8 2.2 %collective-permute-done = bf16[8,9216]{1,0:T(8,128)(2,1)S(1)} collective-permute-done((bf16[8,9216]{1,0:T(8,128)(2,1)S(1)}, bf16[8,9216]{1,0:T(8,128)(2,1)S(1)}, u32[]{:S(2)}, u32[]{:S(2)}) %collective-permute-start) | collective-permute-done | bytes 147488 | tf_op jit(solution)/shard_map/ppermute | solution.py:57
  11.0 1.4 %collective-permute-start.9 = (bf16[16,9216]{1,0:T(8,128)(2,1)S(1)}, bf16[16,9216]{1,0:T(8,128)(2,1)S(1)}, u32[]{:S(2)}, u32[]{:S(2)}) collective-permute-start(bf16[16,9216]{1,0:T(8,128)(2,1)S(1)} %pad_maximum_fusion), channel_id=1, source_target_pairs={{0,16},{1,17},{2,18},{3,19},{4,20},{5,21},{6,22},{7,23},{8,24},{9,... | collective-permute-start | bytes 884744 | tf_op jit(solution)/shard_map/ppermute | solution.py:61
  12.4 2.7 %collective-permute-start.3 = (bf16[8,9216]{1,0:T(8,128)(2,1)S(1)}, bf16[8,9216]{1,0:T(8,128)(2,1)S(1)}, u32[]{:S(2)}, u32[]{:S(2)}) collective-permute-start(bf16[8,9216]{1,0:T(8,128)(2,1)S(1)} %collective-permute-done.1), channel_id=1, source_target_pairs={{0,14},{1,15},{2,0},{3,1},{4,2},{5,3},{6,4},{7,5},{8,6},{9,7},{10,... | collective-permute-start | bytes 442376 | tf_op jit(solution)/shard_map/ppermute | solution.py:58
  15.1 2.5 %collective-permute-done.2 = bf16[8,9216]{1,0:T(8,128)(2,1)S(1)} collective-permute-done((bf16[8,9216]{1,0:T(8,128)(2,1)S(1)}, bf16[8,9216]{1,0:T(8,128)(2,1)S(1)}, u32[]{:S(2)}, u32[]{:S(2)}) %collective-permute-start.2) | collective-permute-done | bytes 147488 | tf_op jit(solution)/shard_map/ppermute | solution.py:57
  17.6 0.0 collective-permute-done.3
  17.6 0.3 collective-permute-start.10
  17.9 1.8 %collective-permute-start.4 = (bf16[8,9216]{1,0:T(8,128)(2,1)S(1)}, bf16[8,9216]{1,0:T(8,128)(2,1)S(1)}, u32[]{:S(2)}, u32[]{:S(2)}) collective-permute-start(bf16[8,9216]{1,0:T(8,128)(2,1)S(1)} %collective-permute-done.2), channel_id=1, source_target_pairs={{0,2},{1,3},{2,4},{3,5},{4,6},{5,7},{6,8},{7,9},{8,10},{9,11},{10,... | collective-permute-start | bytes 442376 | tf_op jit(solution)/shard_map/ppermute | solution.py:57
  19.7 0.8 collective-permute-start.5
  20.6 0.0 copy-start.2
  20.6 0.0 copy-start.3
  20.6 2.5 %collective-permute-done.4 = bf16[8,9216]{1,0:T(8,128)(2,1)S(1)} collective-permute-done((bf16[8,9216]{1,0:T(8,128)(2,1)S(1)}, bf16[8,9216]{1,0:T(8,128)(2,1)S(1)}, u32[]{:S(2)}, u32[]{:S(2)}) %collective-permute-start.4) | collective-permute-done | bytes 147488 | tf_op jit(solution)/shard_map/ppermute | solution.py:57
  23.1 0.6 collective-permute-start.6
  23.7 0.3 collective-permute-done.5
  24.0 1.8 %collective-permute-start.7 = (bf16[8,4608]{1,0:T(8,128)(2,1)S(1)}, bf16[8,4608]{1,0:T(8,128)(2,1)S(1)}, u32[]{:S(2)}, u32[]{:S(2)}) collective-permute-start(bf16[8,4608]{1,0:T(8,128)(2,1)S(1)} %slice.9), channel_id=1, source_target_pairs={{0,14},{1,15},{2,0},{3,1},{4,2},{5,3},{6,4},{7,5},{8,6},{9,7},{10,... | collective-permute-start | bytes 221192 | tf_op jit(solution)/shard_map/ppermute | solution.py:63
  25.9 1.6 %collective-permute-done.6 = bf16[8,4608]{1,0:T(8,128)(2,1)S(1)} collective-permute-done((bf16[8,4608]{1,0:T(8,128)(2,1)S(1)}, bf16[8,4608]{1,0:T(8,128)(2,1)S(1)}, u32[]{:S(2)}, u32[]{:S(2)}) %collective-permute-start.6) | collective-permute-done | bytes 73760 | tf_op jit(solution)/shard_map/ppermute | solution.py:63
  27.5 1.3 collective-permute-start.11
  28.8 0.9 collective-permute-start.12
  29.7 0.0 collective-permute-done.8
  29.8 3.4 %collective-permute-done.11 = bf16[16,9216]{1,0:T(8,128)(2,1)S(1)} collective-permute-done((bf16[16,9216]{1,0:T(8,128)(2,1)S(1)}, bf16[16,9216]{1,0:T(8,128)(2,1)S(1)}, u32[]{:S(2)}, u32[]{:S(2)}) %collective-permute-start.11) | collective-permute-done | bytes 294944 | tf_op jit(solution)/shard_map/ppermute | solution.py:61
  33.3 1.4 %collective-permute-done.12 = bf16[8,9216]{1,0:T(8,128)(2,1)S(1)} collective-permute-done((bf16[8,9216]{1,0:T(8,128)(2,1)S(1)}, bf16[8,9216]{1,0:T(8,128)(2,1)S(1)}, u32[]{:S(2)}, u32[]{:S(2)}) %collective-permute-start.12) | collective-permute-done | bytes 147488 | tf_op jit(solution)/shard_map/ppermute | solution.py:66
  34.7 6.5 %collective-permute-start.13 = (bf16[128,9216]{1,0:T(8,128)(2,1)S(1)}, bf16[128,9216]{1,0:T(8,128)(2,1)S(1)}, u32[]{:S(2)}, u32[]{:S(2)}) collective-permute-start(bf16[128,9216]{1,0:T(8,128)(2,1)S(1)} %constant_dynamic-update-slice_fusion.mine_ref), channel_id=1, source_target_pairs={{0,1},{1,0},{2,3},{3,2},{4,5},{5,4},{6,7},{7,6},{8,9},{9,8},{10,11... | collective-permute-start | bytes 7077896 | tf_op jit(solution)/shard_map/ppermute | solution.py:234
  41.2 4.2 %collective-permute-done.13.other_ref = bf16[128,9216]{1,0:T(8,128)(2,1)S(1)} collective-permute-done((bf16[128,9216]{1,0:T(8,128)(2,1)S(1)}, bf16[128,9216]{1,0:T(8,128)(2,1)S(1)}, u32[]{:S(2)}, u32[]{:S(2)}) %collective-permute-start.13) | collective-permute-done | bytes 2359328 | tf_op jit(solution)/shard_map/ppermute | solution.py:234
  45.4 9.5 %rhs_rows.1 = f32[256,512]{1,0:T(8,128)S(1)} custom-call(bf16[128,9216]{1,0:T(8,128)(2,1)S(1)} %constant_dynamic-update-slice_fusion.mine_ref, bf16[128,9216]{1,0:T(8,128)(2,1)S(1)} %collective-permute-done.13.other_ref, bf16[6144,512]{1,0:T(8,128)(2,1)} %rate_ref.1, s32[6,8,512]{2,1,0:T(8,128)S(1)} %bitcast.36, bf16[3072,512]{1,0:T(8,128)(2,1)} %attr_ref.1, ...), custom_call_target="tpu_custom_call" | custom-call | tf_op jit(solution)/shard_map/rhs_rows/pallas_call | solution.py:130
  54.9 2.6 %collective-permute-start.14 = (f32[256,512]{1,0:T(8,128)S(1)}, f32[256,512]{1,0:T(8,128)S(1)}, u32[]{:S(2)}, u32[]{:S(2)}) collective-permute-start(f32[256,512]{1,0:T(8,128)S(1)} %rhs_rows.1), channel_id=1, source_target_pairs={{0,32},{1,97},{2,34},{3,99},{4,36},{5,101},{6,38},{7,103},{8,40},{... | collective-permute-start | bytes 1572872 | tf_op jit(solution)/shard_map/ppermute | solution.py:227
  57.5 6.8 %collective-permute-done.14 = f32[256,512]{1,0:T(8,128)S(1)} collective-permute-done((f32[256,512]{1,0:T(8,128)S(1)}, f32[256,512]{1,0:T(8,128)S(1)}, u32[]{:S(2)}, u32[]{:S(2)}) %collective-permute-start.14) | collective-permute-done | bytes 524320 | tf_op jit(solution)/shard_map/ppermute | solution.py:227
  64.2 0.1 add.382
  64.3 0.4 collective-permute-start.15
  64.7 7.4 %top_gram.1 = f32[128,256]{1,0:T(8,128)} custom-call(bf16[128,9216]{1,0:T(8,128)(2,1)} %copy-done, bf16[128,9216]{1,0:T(8,128)(2,1)} %copy-done.1), custom_call_target="tpu_custom_call" | custom-call | tf_op jit(solution)/shard_map/top_gram/pallas_call | solution.py:87
  72.1 2.2 %collective-permute-start.17 = (f32[128,256]{1,0:T(8,128)}, f32[128,256]{1,0:T(8,128)S(1)}, u32[]{:S(2)}, u32[]{:S(2)}) collective-permute-start(f32[128,256]{1,0:T(8,128)} %top_gram.1), channel_id=1, source_target_pairs={{0,32},{1,97},{2,34},{3,99},{4,36},{5,101},{6,38},{7,103},{8,40},{... | collective-permute-start | bytes 393224 | tf_op jit(solution)/shard_map/ppermute | solution.py:227
  74.3 0.1 add.383.rhs_ref
  74.4 3.0 %collective-permute-start.16 = (f32[256,512]{1,0:T(8,128)S(1)}, f32[256,512]{1,0:T(8,128)S(1)}, u32[]{:S(2)}, u32[]{:S(2)}) collective-permute-start(f32[256,512]{1,0:T(8,128)S(1)} %add.383.rhs_ref), channel_id=1, source_target_pairs={{0,128},{1,129},{2,130},{3,131},{4,132},{5,133},{6,134},{7,135},{8... | collective-permute-start | bytes 1572872 | tf_op jit(solution)/shard_map/ppermute | solution.py:253
  77.4 0.9 add.455
  78.4 0.9 collective-permute-start.18
  79.3 3.3 %collective-permute-done.18 = f32[128,256]{1,0:T(8,128)S(1)} collective-permute-done((f32[128,256]{1,0:T(8,128)S(1)}, f32[128,256]{1,0:T(8,128)S(1)}, u32[]{:S(2)}, u32[]{:S(2)}) %collective-permute-start.18) | collective-permute-done | bytes 131104 | tf_op jit(solution)/shard_map/ppermute | solution.py:227
  82.6 2.9 %collective-permute-start.19 = (f32[128,256]{1,0:T(8,128)S(1)}, f32[128,256]{1,0:T(8,128)S(1)}, u32[]{:S(2)}, u32[]{:S(2)}) collective-permute-start(f32[128,256]{1,0:T(8,128)S(1)} %add.456), channel_id=1, source_target_pairs={{0,128},{1,129},{2,130},{3,131},{4,132},{5,133},{6,134},{7,135},{8... | collective-permute-start | bytes 393224 | tf_op jit(solution)/shard_map/ppermute | solution.py:227
  85.5 5.7 %collective-permute-done.19 = f32[128,256]{1,0:T(8,128)S(1)} collective-permute-done((f32[128,256]{1,0:T(8,128)S(1)}, f32[128,256]{1,0:T(8,128)S(1)}, u32[]{:S(2)}, u32[]{:S(2)}) %collective-permute-start.19) | collective-permute-done | bytes 131104 | tf_op jit(solution)/shard_map/ppermute | solution.py:227
  91.3 0.0 copy-start.6
  91.3 2.7 %collective-permute-start.20 = (f32[128,256]{1,0:T(8,128)S(1)}, f32[128,256]{1,0:T(8,128)S(1)}, u32[]{:S(2)}, u32[]{:S(2)}) collective-permute-start(f32[128,256]{1,0:T(8,128)S(1)} %add.457.top_ref), channel_id=1, source_target_pairs={{0,1},{1,0},{2,3},{3,2},{4,5},{5,4},{6,7},{7,6},{8,9},{9,8},{10,11... | collective-permute-start | bytes 393224 | tf_op jit(solution)/shard_map/ppermute | solution.py:249
  94.0 0.7 stack.131.order_ref
  94.7 0.3 collective-permute-done.20.peer_ref
  95.0 0.7 copy-done.7
  95.6 38.1 %ordered_inverse.1.inverse_ref = f32[256,256]{1,0:T(8,128)} custom-call(s32[32]{0:T(128)} %stack.131.order_ref, f32[128,256]{1,0:T(8,128)} %copy-done.6, f32[128,256]{1,0:T(8,128)} %copy-done.7), custom_call_target="tpu_custom_call" | custom-call | tf_op jit(solution)/shard_map/ordered_inverse/pallas_call | solution.py:192
  133.8 0.8 copy-done.5
  134.6 2.7 %final_solve.1 = f32[512,256]{1,0:T(8,128)} custom-call(f32[256,512]{1,0:T(8,128)} %copy-done.4, f32[256,512]{1,0:T(8,128)} %copy-done.5, f32[256,256]{1,0:T(8,128)} %ordered_inverse.1.inverse_ref), custom_call_target="tpu_custom_call" | custom-call | tf_op jit(solution)/shard_map/final_solve/pallas_call | solution.py:219
  (40 shorter events, 0.3 us)
Async XLA Ops:
  0.9 10.1 %collective-permute-start = (bf16[8,9216]{1,0:T(8,128)(2,1)S(1)}, bf16[8,9216]{1,0:T(8,128)(2,1)S(1)}, u32[]{:S(2)}, u32[]{:S(2)}) collective-permute-start(bf16[8,9216]{1,0:T(8,128)(2,1)S(1)} %get-tuple-element.5), channel_id=1, source_target_pairs={{0,2},{1,3},{2,4},{3,5},{4,6},{5,7},{6,8},{7,9},{8,10},{9,11},{10,... | collective-permute-start | bytes 442376 | tf_op jit(solution)/shard_map/ppermute | solution.py:57
  3.5 7.5 %collective-permute-start.1 = (bf16[8,9216]{1,0:T(8,128)(2,1)S(1)}, bf16[8,9216]{1,0:T(8,128)(2,1)S(1)}, u32[]{:S(2)}, u32[]{:S(2)}) collective-permute-start(bf16[8,9216]{1,0:T(8,128)(2,1)S(1)} %get-tuple-element.5), channel_id=1, source_target_pairs={{0,14},{1,15},{2,0},{3,1},{4,2},{5,3},{6,4},{7,5},{8,6},{9,7},{10,... | collective-permute-start | bytes 442376 | tf_op jit(solution)/shard_map/ppermute | solution.py:58
  7.5 22.2 %collective-permute-start.8 = (bf16[8,9216]{1,0:T(8,128)(2,1)S(1)}, bf16[8,9216]{1,0:T(8,128)(2,1)S(1)}, u32[]{:S(2)}, u32[]{:S(2)}) collective-permute-start(bf16[8,9216]{1,0:T(8,128)(2,1)S(1)} %get-tuple-element.5), channel_id=1, source_target_pairs={{0,16},{1,17},{2,18},{3,19},{4,20},{5,21},{6,22},{7,23},{8,24},{9,... | collective-permute-start | bytes 442376 | tf_op jit(solution)/shard_map/ppermute | solution.py:55
  11.0 18.7 %collective-permute-start.9 = (bf16[16,9216]{1,0:T(8,128)(2,1)S(1)}, bf16[16,9216]{1,0:T(8,128)(2,1)S(1)}, u32[]{:S(2)}, u32[]{:S(2)}) collective-permute-start(bf16[16,9216]{1,0:T(8,128)(2,1)S(1)} %pad_maximum_fusion), channel_id=1, source_target_pairs={{0,16},{1,17},{2,18},{3,19},{4,20},{5,21},{6,22},{7,23},{8,24},{9,... | collective-permute-start | bytes 884744 | tf_op jit(solution)/shard_map/ppermute | solution.py:61
  12.4 5.2 %collective-permute-start.2 = (bf16[8,9216]{1,0:T(8,128)(2,1)S(1)}, bf16[8,9216]{1,0:T(8,128)(2,1)S(1)}, u32[]{:S(2)}, u32[]{:S(2)}) collective-permute-start(bf16[8,9216]{1,0:T(8,128)(2,1)S(1)} %collective-permute-done), channel_id=1, source_target_pairs={{0,2},{1,3},{2,4},{3,5},{4,6},{5,7},{6,8},{7,9},{8,10},{9,11},{10,... | collective-permute-start | bytes 442376 | tf_op jit(solution)/shard_map/ppermute | solution.py:57
  12.4 5.2 %collective-permute-start.3 = (bf16[8,9216]{1,0:T(8,128)(2,1)S(1)}, bf16[8,9216]{1,0:T(8,128)(2,1)S(1)}, u32[]{:S(2)}, u32[]{:S(2)}) collective-permute-start(bf16[8,9216]{1,0:T(8,128)(2,1)S(1)} %collective-permute-done.1), channel_id=1, source_target_pairs={{0,14},{1,15},{2,0},{3,1},{4,2},{5,3},{6,4},{7,5},{8,6},{9,7},{10,... | collective-permute-start | bytes 442376 | tf_op jit(solution)/shard_map/ppermute | solution.py:58
  17.6 12.2 %collective-permute-start.10 = (bf16[16,9216]{1,0:T(8,128)(2,1)S(1)}, bf16[16,9216]{1,0:T(8,128)(2,1)S(1)}, u32[]{:S(2)}, u32[]{:S(2)}) collective-permute-start(bf16[16,9216]{1,0:T(8,128)(2,1)S(1)} %pad_maximum_fusion.1), channel_id=1, source_target_pairs={{0,16},{1,17},{2,18},{3,19},{4,20},{5,21},{6,22},{7,23},{8,24},{9,... | collective-permute-start | bytes 884744 | tf_op jit(solution)/shard_map/ppermute | solution.py:61
  17.9 5.2 %collective-permute-start.4 = (bf16[8,9216]{1,0:T(8,128)(2,1)S(1)}, bf16[8,9216]{1,0:T(8,128)(2,1)S(1)}, u32[]{:S(2)}, u32[]{:S(2)}) collective-permute-start(bf16[8,9216]{1,0:T(8,128)(2,1)S(1)} %collective-permute-done.2), channel_id=1, source_target_pairs={{0,2},{1,3},{2,4},{3,5},{4,6},{5,7},{6,8},{7,9},{8,10},{9,11},{10,... | collective-permute-start | bytes 442376 | tf_op jit(solution)/shard_map/ppermute | solution.py:57
  19.7 4.3 %collective-permute-start.5 = (bf16[8,9216]{1,0:T(8,128)(2,1)S(1)}, bf16[8,9216]{1,0:T(8,128)(2,1)S(1)}, u32[]{:S(2)}, u32[]{:S(2)}) collective-permute-start(bf16[8,9216]{1,0:T(8,128)(2,1)S(1)} %collective-permute-done.3), channel_id=1, source_target_pairs={{0,14},{1,15},{2,0},{3,1},{4,2},{5,3},{6,4},{7,5},{8,6},{9,7},{10,... | collective-permute-start | bytes 442376 | tf_op jit(solution)/shard_map/ppermute | solution.py:58
  20.6 24.7 %copy-start.2 = (s32[48,512]{1,0:T(8,128)S(1)}, s32[48,512]{1,0:T(8,128)}, u32[]{:S(2)}) copy-start(s32[48,512]{1,0:T(8,128)} %param.7) | copy-start | bytes 294916
  20.6 24.7 %copy-start.3 = (s32[24,512]{1,0:T(8,128)S(1)}, s32[24,512]{1,0:T(8,128)}, u32[]{:S(2)}) copy-start(s32[24,512]{1,0:T(8,128)} %param.9) | copy-start | bytes 147460
  23.1 4.4 %collective-permute-start.6 = (bf16[8,4608]{1,0:T(8,128)(2,1)S(1)}, bf16[8,4608]{1,0:T(8,128)(2,1)S(1)}, u32[]{:S(2)}, u32[]{:S(2)}) collective-permute-start(bf16[8,4608]{1,0:T(8,128)(2,1)S(1)} %slice.8), channel_id=1, source_target_pairs={{0,2},{1,3},{2,4},{3,5},{4,6},{5,7},{6,8},{7,9},{8,10},{9,11},{10,... | collective-permute-start | bytes 221192 | tf_op jit(solution)/shard_map/ppermute | solution.py:63
  24.0 4.8 %collective-permute-start.7 = (bf16[8,4608]{1,0:T(8,128)(2,1)S(1)}, bf16[8,4608]{1,0:T(8,128)(2,1)S(1)}, u32[]{:S(2)}, u32[]{:S(2)}) collective-permute-start(bf16[8,4608]{1,0:T(8,128)(2,1)S(1)} %slice.9), channel_id=1, source_target_pairs={{0,14},{1,15},{2,0},{3,1},{4,2},{5,3},{6,4},{7,5},{8,6},{9,7},{10,... | collective-permute-start | bytes 221192 | tf_op jit(solution)/shard_map/ppermute | solution.py:63
  27.5 5.8 %collective-permute-start.11 = (bf16[16,9216]{1,0:T(8,128)(2,1)S(1)}, bf16[16,9216]{1,0:T(8,128)(2,1)S(1)}, u32[]{:S(2)}, u32[]{:S(2)}) collective-permute-start(bf16[16,9216]{1,0:T(8,128)(2,1)S(1)} %pad_maximum_fusion.2), channel_id=1, source_target_pairs={{0,16},{1,17},{2,18},{3,19},{4,20},{5,21},{6,22},{7,23},{8,24},{9,... | collective-permute-start | bytes 884744 | tf_op jit(solution)/shard_map/ppermute | solution.py:61
  28.8 5.8 %collective-permute-start.12 = (bf16[8,9216]{1,0:T(8,128)(2,1)S(1)}, bf16[8,9216]{1,0:T(8,128)(2,1)S(1)}, u32[]{:S(2)}, u32[]{:S(2)}) collective-permute-start(bf16[8,9216]{1,0:T(8,128)(2,1)S(1)} %pad_maximum_fusion.3), channel_id=1, source_target_pairs={{0,16},{1,17},{2,18},{3,19},{4,20},{5,21},{6,22},{7,23},{8,24},{9,... | collective-permute-start | bytes 442376 | tf_op jit(solution)/shard_map/ppermute | solution.py:66
  34.7 20.2 %copy-start = (bf16[128,9216]{1,0:T(8,128)(2,1)}, bf16[128,9216]{1,0:T(8,128)(2,1)S(1)}, u32[]{:S(2)}) copy-start(bf16[128,9216]{1,0:T(8,128)(2,1)S(1)} %constant_dynamic-update-slice_fusion.mine_ref) | copy-start | bytes 7077892
  34.7 10.6 %collective-permute-start.13 = (bf16[128,9216]{1,0:T(8,128)(2,1)S(1)}, bf16[128,9216]{1,0:T(8,128)(2,1)S(1)}, u32[]{:S(2)}, u32[]{:S(2)}) collective-permute-start(bf16[128,9216]{1,0:T(8,128)(2,1)S(1)} %constant_dynamic-update-slice_fusion.mine_ref), channel_id=1, source_target_pairs={{0,1},{1,0},{2,3},{3,2},{4,5},{5,4},{6,7},{7,6},{8,9},{9,8},{10,11... | collective-permute-start | bytes 7077896 | tf_op jit(solution)/shard_map/ppermute | solution.py:234
  45.3 9.6 %copy-start.1 = (bf16[128,9216]{1,0:T(8,128)(2,1)}, bf16[128,9216]{1,0:T(8,128)(2,1)S(1)}, u32[]{:S(2)}) copy-start(bf16[128,9216]{1,0:T(8,128)(2,1)S(1)} %collective-permute-done.13.other_ref) | copy-start | bytes 7077892
  54.9 9.3 %collective-permute-start.14 = (f32[256,512]{1,0:T(8,128)S(1)}, f32[256,512]{1,0:T(8,128)S(1)}, u32[]{:S(2)}, u32[]{:S(2)}) collective-permute-start(f32[256,512]{1,0:T(8,128)S(1)} %rhs_rows.1), channel_id=1, source_target_pairs={{0,32},{1,97},{2,34},{3,99},{4,36},{5,101},{6,38},{7,103},{8,40},{... | collective-permute-start | bytes 1572872 | tf_op jit(solution)/shard_map/ppermute | solution.py:227
  64.3 10.0 %collective-permute-start.15 = (f32[256,512]{1,0:T(8,128)S(1)}, f32[256,512]{1,0:T(8,128)S(1)}, u32[]{:S(2)}, u32[]{:S(2)}) collective-permute-start(f32[256,512]{1,0:T(8,128)S(1)} %add.382), channel_id=1, source_target_pairs={{0,96},{1,33},{2,98},{3,35},{4,100},{5,37},{6,102},{7,39},{8,104},... | collective-permute-start | bytes 1572872 | tf_op jit(solution)/shard_map/ppermute | solution.py:227
  72.1 5.3 %collective-permute-start.17 = (f32[128,256]{1,0:T(8,128)}, f32[128,256]{1,0:T(8,128)S(1)}, u32[]{:S(2)}, u32[]{:S(2)}) collective-permute-start(f32[128,256]{1,0:T(8,128)} %top_gram.1), channel_id=1, source_target_pairs={{0,32},{1,97},{2,34},{3,99},{4,36},{5,101},{6,38},{7,103},{8,40},{... | collective-permute-start | bytes 393224 | tf_op jit(solution)/shard_map/ppermute | solution.py:227
  74.4 59.3 %copy-start.4 = (f32[256,512]{1,0:T(8,128)}, f32[256,512]{1,0:T(8,128)S(1)}, u32[]{:S(2)}) copy-start(f32[256,512]{1,0:T(8,128)S(1)} %add.383.rhs_ref) | copy-start | bytes 1572868
  74.4 59.3 %collective-permute-start.16 = (f32[256,512]{1,0:T(8,128)S(1)}, f32[256,512]{1,0:T(8,128)S(1)}, u32[]{:S(2)}, u32[]{:S(2)}) collective-permute-start(f32[256,512]{1,0:T(8,128)S(1)} %add.383.rhs_ref), channel_id=1, source_target_pairs={{0,128},{1,129},{2,130},{3,131},{4,132},{5,133},{6,134},{7,135},{8... | collective-permute-start | bytes 1572872 | tf_op jit(solution)/shard_map/ppermute | solution.py:253
  78.4 4.2 %collective-permute-start.18 = (f32[128,256]{1,0:T(8,128)S(1)}, f32[128,256]{1,0:T(8,128)S(1)}, u32[]{:S(2)}, u32[]{:S(2)}) collective-permute-start(f32[128,256]{1,0:T(8,128)S(1)} %add.455), channel_id=1, source_target_pairs={{0,96},{1,33},{2,98},{3,35},{4,100},{5,37},{6,102},{7,39},{8,104},... | collective-permute-start | bytes 393224 | tf_op jit(solution)/shard_map/ppermute | solution.py:227
  82.6 8.7 %collective-permute-start.19 = (f32[128,256]{1,0:T(8,128)S(1)}, f32[128,256]{1,0:T(8,128)S(1)}, u32[]{:S(2)}, u32[]{:S(2)}) collective-permute-start(f32[128,256]{1,0:T(8,128)S(1)} %add.456), channel_id=1, source_target_pairs={{0,128},{1,129},{2,130},{3,131},{4,132},{5,133},{6,134},{7,135},{8... | collective-permute-start | bytes 393224 | tf_op jit(solution)/shard_map/ppermute | solution.py:227
  91.3 3.7 %copy-start.6 = (f32[128,256]{1,0:T(8,128)}, f32[128,256]{1,0:T(8,128)S(1)}, u32[]{:S(2)}) copy-start(f32[128,256]{1,0:T(8,128)S(1)} %add.457.top_ref) | copy-start | bytes 393220
  91.3 3.7 %collective-permute-start.20 = (f32[128,256]{1,0:T(8,128)S(1)}, f32[128,256]{1,0:T(8,128)S(1)}, u32[]{:S(2)}, u32[]{:S(2)}) collective-permute-start(f32[128,256]{1,0:T(8,128)S(1)} %add.457.top_ref), channel_id=1, source_target_pairs={{0,1},{1,0},{2,3},{3,2},{4,5},{5,4},{6,7},{7,6},{8,9},{9,8},{10,11... | collective-permute-start | bytes 393224 | tf_op jit(solution)/shard_map/ppermute | solution.py:249
  95.0 0.7 copy-start.7
  133.8 0.8 copy-start.5

commit v2 on v0

v2 whole, which is shorter than its diff:
```python
import functools

import jax
import jax.numpy as jnp
from jax import lax
from jax.experimental import pallas as pl
from jax.experimental.pallas import tpu as pltpu
from jax.sharding import PartitionSpec as P

LAMBDA = 0.5
REG = 0.1
SUB = 8
BLOCK = 32

NY, NZ, NC = 2, 8, 2
NYH, NX = 2, 4
NT = (((1,), (1,)), ((), ()))


def item_of(y, z, c):
    return ((y % NY) * NZ + z % NZ) * NC + c % NC


def item_perm(dy, dz, dc):
    places = [(y, z, c) for y in range(NY) for z in range(NZ) for c in range(NC)]
    return [(item_of(y, z, c), item_of(y + dy, z + dz, c + dc)) for y, z, c in places]


def band_perm(stage):
    pairs = []
    for yh in range(NYH):
        for x in range(NX):
            for item in range(NY * NZ * NC):
                if stage == 2:
                    to = (1 - yh) * NX + x
                elif stage == item % NC:
                    to = yh * NX + (x ^ 1)
                else:
                    to = yh * NX + (NX - 1 - x)
                pairs.append(((yh * NX + x) * 32 + item, to * 32 + item))
    return pairs


UP = item_perm(0, 1, 0)
DOWN = item_perm(0, -1, 0)
ACROSS = item_perm(1, 0, 0)
CORE = item_perm(0, 0, 1)


def gather_columns(own):
    half = own.shape[1] // 2
    up = down = own
    near, far = [own], []
    pending = own
    for step in range(1, 4):
        far.append(lax.ppermute(pending, "item", ACROSS))
        down = lax.ppermute(down, "item", DOWN)
        up = lax.ppermute(up, "item", UP)
        pending = jnp.concatenate([up, down], axis=0)
        near.append(pending)
    far.append(lax.ppermute(pending, "item", ACROSS))
    last = jnp.concatenate(
        [lax.ppermute(up[:, :half], "item", UP), lax.ppermute(down[:, half:], "item", DOWN)], axis=1
    )
    first_part = near + far[:3]
    second_part = [last, far[3], lax.ppermute(last, "item", ACROSS)]
    return jnp.concatenate(first_part, axis=0), jnp.concatenate(second_part, axis=0)


PLACES = [(0, dz) for dz in (0, -1, 1, -2, 2, -3, 3)] + [(1, dz) for dz in (0, -1, 1, -2, 2)]
PLACES += [(0, 4), (1, -3), (1, 3), (1, 4)]


def whole():
    return pl.BlockSpec(memory_space=pltpu.VMEM)


def mask_kernel(scale, value_ref, mask_ref, out_ref):
    for block in range(mask_ref.shape[0]):
        rows = slice(block * 128, (block + 1) * 128)
        keep = (mask_ref[block : block + 1, :].astype(jnp.float32) * scale).astype(jnp.bfloat16)
        out_ref[rows, :] = value_ref[rows, :] * keep


def masked(values, mask, scale, name):
    return pl.pallas_call(
        functools.partial(mask_kernel, scale),
        out_shape=jax.ShapeDtypeStruct(values.shape, values.dtype),
        in_specs=[whole(), whole()],
        out_specs=whole(),
        compiler_params=pltpu.CompilerParams(vmem_limit_bytes=4 << 20),
        name=name,
    )(values, mask)


def weighted_gram(left_ref, right_ref, users):
    total = lax.dot_general(left_ref[:, :users], right_ref[:, :users], NT, preferred_element_type=jnp.float32)
    tags = lax.dot_general(left_ref[:, users:], right_ref[:, users:], NT, preferred_element_type=jnp.float32)
    return total + LAMBDA * tags


def gram_kernel(users, mine_ref, other_ref, out_ref):
    out_ref[:, :128] = weighted_gram(mine_ref, mine_ref, users)
    out_ref[:, 128:] = weighted_gram(mine_ref, other_ref, users)


def top_gram(mine, other, n_users):
    return pl.pallas_call(
        functools.partial(gram_kernel, n_users),
        out_shape=jax.ShapeDtypeStruct((128, 256), jnp.float32),
        in_specs=[whole(), whole()],
        out_specs=whole(),
        compiler_params=pltpu.CompilerParams(vmem_limit_bytes=4 << 20),
        name="top_gram",
    )(mine, other)


def rhs_kernel(factor_ref, *refs):
    parts, out_ref = refs[:-1], refs[-1]
    start = 0
    total = None
    for part_ref in parts:
        rows = part_ref.shape[0]
        product = jnp.dot(factor_ref[:, start : start + rows], part_ref[...], preferred_element_type=jnp.float32)
        total = product if total is None else total + product
        start += rows
    out_ref[...] = total


def rhs_rows(factor, parts, name):
    return pl.pallas_call(
        rhs_kernel,
        out_shape=jax.ShapeDtypeStruct((factor.shape[0], parts[0].shape[1]), jnp.float32),
        in_specs=[whole()] * (1 + len(parts)),
        out_specs=whole(),
        compiler_params=pltpu.CompilerParams(vmem_limit_bytes=4 << 20),
        name=name,
    )(factor, *parts)


def spread(x):
    return jnp.broadcast_to(x, (SUB, 128))


def small_inverse(columns, sub):
    for j in range(SUB):
        hit = sub == j
        pivot = columns[j]
        inv = 1.0 / spread(pivot[j : j + 1, :])
        new = []
        for m in range(SUB):
            if m == j:
                new.append(jnp.where(hit, inv, -pivot * inv))
            else:
                row = spread(columns[m][j : j + 1, :]) * inv
                new.append(jnp.where(hit, row, columns[m] - pivot * row))
        columns = new
    return columns


def weighted_rows(weights, rows):
    total = weights[0] * rows[0]
    for weight, row in zip(weights[1:], rows[1:]):
        total = total + weight * row
    return total


def inverse_kernel(order_ref, top_ref, peer_ref, out_ref, a_ref):
    n = a_ref.shape[0]
    h = n // 2
    a_ref[:h, :] = top_ref[...]
    a_ref[h:, :h] = peer_ref[:, h:]
    a_ref[h:, h:] = peer_ref[:, :h]
    sub = lax.broadcasted_iota(jnp.int32, (SUB, 128), 0)
    lane = lax.broadcasted_iota(jnp.int32, (SUB, 128), 1)
    wide = lax.broadcasted_iota(jnp.int32, (1, 128), 1)
    for r in range(0, n, SUB):
        at = slice(r // 128 * 128, r // 128 * 128 + 128)
        a_ref[r : r + SUB, at] += jnp.where(lane == sub + r % 128, REG, 0.0)

    panels = BLOCK // SUB
    ahead = None
    for r0 in range(0, n, BLOCK):
        side = r0 // 128
        base = r0 % 128
        panel = []
        for q in range(panels):
            rows = slice(r0 + q * SUB, r0 + (q + 1) * SUB)
            panel.append([a_ref[rows, :128], a_ref[rows, 128:]])
        if ahead is not None:
            panel[0] = ahead
        for q in range(panels):
            k = base + q * SUB
            inside = (lane >= k) & (lane < k + SUB)
            small = small_inverse([spread(panel[q][side][:, k + m : k + m + 1]) for m in range(SUB)], sub)
            fresh = []
            for s in range(2):
                value = weighted_rows(small, [spread(panel[q][s][m : m + 1, :]) for m in range(SUB)])
                if s == side:
                    for m in range(SUB):
                        value = jnp.where(lane == k + m, small[m], value)
                fresh.append(value)
            panel[q] = fresh
            rows = [[spread(fresh[s][m : m + 1, :]) for m in range(SUB)] for s in range(2)]
            for i in range(panels):
                if i == q:
                    continue
                left = [spread(panel[i][side][:, k + m : k + m + 1]) for m in range(SUB)]
                for s in range(2):
                    old = panel[i][s]
                    if s == side:
                        old = jnp.where(inside, 0.0, old)
                    panel[i][s] = old - weighted_rows(left, rows[s])
        block = jnp.concatenate([jnp.concatenate(panel[q], axis=1) for q in range(panels)], axis=0)
        r1 = r0 + BLOCK
        if r1 < n:
            left = [spread(a_ref[r1 : r1 + SUB, r0 + m : r0 + m + 1]) for m in range(BLOCK)]
            ahead = []
            for s in range(2):
                old = a_ref[r1 : r1 + SUB, s * 128 : (s + 1) * 128]
                if s == side:
                    old = jnp.where((lane >= base) & (lane < base + BLOCK), 0.0, old)
                for q in range(panels):
                    rows = [spread(panel[q][s][m : m + 1, :]) for m in range(SUB)]
                    old = old - weighted_rows(left[q * SUB : (q + 1) * SUB], rows)
                ahead.append(old)
        change = jnp.dot(a_ref[:, r0:r1], block, preferred_element_type=jnp.float32, precision=lax.Precision.HIGHEST)
        for s in range(2):
            at = slice(s * 128, (s + 1) * 128)
            old = a_ref[:, at]
            if s == side:
                old = jnp.where((wide >= base) & (wide < base + BLOCK), 0.0, old)
            a_ref[:, at] = old - change[:, at]
        a_ref[r0:r1, :] = block

    for b in range(n // 8):
        out_ref[pl.ds(pl.multiple_of(order_ref[b] * 8, 8), 8), :] = a_ref[b * 8 : (b + 1) * 8, :]


def ordered_inverse(order, top, peer):
    n = top.shape[1]
    return pl.pallas_call(
        inverse_kernel,
        out_shape=jax.ShapeDtypeStruct((n, n), jnp.float32),
        in_specs=[pl.BlockSpec(memory_space=pltpu.SMEM), whole(), whole()],
        out_specs=whole(),
        scratch_shapes=[pltpu.VMEM((n, n), jnp.float32)],
        compiler_params=pltpu.CompilerParams(vmem_limit_bytes=4 << 20),
        cost_estimate=pl.CostEstimate(flops=3 * 10**10, bytes_accessed=10**8, transcendentals=0),
        name="ordered_inverse",
    )(order, top, peer)


def final_kernel(rhs_ref, more_ref, inverse_ref, out_ref):
    out_ref[...] = lax.dot_general(
        rhs_ref[...] + more_ref[...],
        inverse_ref[...],
        (((0,), (1,)), ((), ())),
        preferred_element_type=jnp.float32,
        precision=lax.Precision.HIGHEST,
    )


def final_solve(*values):
    k, items = values[0].shape
    return pl.pallas_call(
        final_kernel,
        out_shape=jax.ShapeDtypeStruct((items, k), jnp.float32),
        in_specs=[whole()] * len(values),
        out_specs=whole(),
        compiler_params=pltpu.CompilerParams(vmem_limit_bytes=8 << 20),
        name="final_solve",
    )(*values)


def swap(value, stage):
    return lax.ppermute(value, ("band", "item"), band_perm(stage))


def body(ratings, rating_mask, attributes, attribute_mask, user_factors, tag_factors):
    n_users = user_factors.shape[0]
    own = jnp.concatenate([user_factors.T, tag_factors.T], axis=1)
    first, second = gather_columns(own)
    other_first = lax.ppermute(first, "item", CORE)
    other_second = lax.ppermute(second, "item", CORE)
    mine = jnp.concatenate([first, second], axis=0)
    other = jnp.concatenate([other_first, other_second], axis=0)

    parts = [
        masked(ratings, rating_mask, 1.0, "mask_users"),
        masked(attributes, attribute_mask, LAMBDA, "mask_tags"),
    ]

    item = lax.axis_index("item")
    y, z, c = item // (NZ * NC), (item // NC) % NZ, item % NC
    dc = jnp.repeat(jnp.arange(2, dtype=jnp.int32), 16)
    dy = jnp.array([p[0] for p in PLACES] * 2, jnp.int32)
    dz = jnp.array([p[1] + NZ for p in PLACES] * 2, jnp.int32)
    order = (((y + dy) % NY) * NZ + (z + dz) % NZ) * NC + (c + dc) % NC

    rhs_mine = rhs_rows(mine, parts, "rhs_mine")
    top = top_gram(mine, other, n_users)
    top, later = lax.optimization_barrier((top, other))
    rhs_other = rhs_rows(later, parts, "rhs_other")

    fresh, peer_mine, rhs_other = lax.optimization_barrier((swap(top, 0), swap(rhs_mine, 0), rhs_other))
    top = top + fresh
    rhs_mine = rhs_mine + peer_mine
    fresh, peer_other = lax.optimization_barrier((swap(top, 1), swap(rhs_other, 0)))
    top = top + fresh
    rhs = jnp.concatenate([rhs_mine, rhs_other + peer_other], axis=0)
    rhs = rhs + swap(rhs, 1)
    top = top + swap(top, 2)
    inverse = ordered_inverse(order, top, lax.ppermute(top, "item", CORE))
    return final_solve(rhs, swap(rhs, 2), inverse)


def solution(mesh):
    spec = P("band", "item")
    return jax.shard_map(
        body, mesh=mesh, in_specs=(spec,) * 6, out_specs=P("item", None), check_vma=False
    )
```

time: 317 us -> 83.7 us (0.26); the launches traced: 313 us -> 83.4 us
  waiting for transfers between devices: 213 us -> 20.6 us
  other arithmetic: 63 us -> 1.34 us
  starting transfers between devices: 0.08 us -> 42.6 us
  Pallas kernels: 0 us -> 17.9 us
  matrix products: 16 us -> 0 us
  between operations: 14.6 us -> 0.34 us
  local copies, waits for them, and re-layouts: 6.6 us -> 0.62 us
    all_gather x2 -> x0, waiting for transfers between devices: 126 us -> none  [the longest x1 64.4 us: body(): users = lax.all_gather(user_factors, 'item', axis=1, tiled=True)]
    psum x1 -> x0, waiting for transfers between devices: 85.5 us -> none  [body(): summed_rhs = lax.psum(local_rhs, 'band')]
    another operation x10 -> x0, other arithmetic: 53.9 us -> none  [the longest x6 34.1 us: finish_gram(): jnp.linalg.cholesky(summed_gram + REG * jnp.eye(rank, dtype=jnp.float32))]
    ppermute x0 -> x23, starting transfers between devices: none -> 42.6 us  [the longest x7 10.4 us: swap(): return lax.ppermute(value, ('band', 'item'), band_perm(stage))]
    ppermute x0 -> x23, waiting for transfers between devices: none -> 20.6 us  [the longest x7 12.3 us: swap(): return lax.ppermute(value, ('band', 'item'), band_perm(stage))]
    pallas_call x0 -> x7, Pallas kernels: none -> 17.9 us  [the longest x1 11.6 us: ordered_inverse(): pl.pallas_call(inverse_kernel, out_shape=jax.ShapeDtypeStruct((n, n), jnp...]
    dot_general x4 -> x0, matrix products: 13 us -> none  [inner(): lax.dot_general(left, right, (((0,), (0,)), ((), ())), preferred_element_...]
    mul x2 -> x0, other arithmetic: 5.35 us -> none  [apply_mask(): values.reshape(blocks, rows // blocks, cols)]
  transfers between devices with their start and end apart: 3 -> 23, of which waited for: 3 -> 10; matrix products, arithmetic and copies ran while one was open for 3% -> 1% of each run, Pallas kernels for 0% -> 20%
where the time goes in v2:
time: 83.7 us; the launch traced here: 83.4 us
  starting transfers between devices  42.6 us (51%)
  waiting for transfers between devices  20.6 us (25%)
  Pallas kernels  17.9 us (21%)
  other arithmetic  1.34 us (2%)
    ppermute x7, waiting for transfers between devices, swap(): return lax.ppermute(value, ('band', 'item'), band_perm(stage))  12.3 us
    pallas_call x1, Pallas kernels, ordered_inverse(): pl.pallas_call(inverse_kernel, out_shape=jax.ShapeDtypeStruct((n, n), jnp...  11.6 us
    ppermute x7, starting transfers between devices, swap(): return lax.ppermute(value, ('band', 'item'), band_perm(stage))  10.4 us
    ppermute x3, starting transfers between devices, gather_columns(): down = lax.ppermute(down, 'item', DOWN)  7.55 us
    ppermute x3, waiting for transfers between devices, gather_columns(): up = lax.ppermute(up, 'item', UP)  7.12 us
    ppermute x1, starting transfers between devices, body(): other_first = lax.ppermute(first, 'item', CORE)  5.69 us
    ppermute x3, starting transfers between devices, gather_columns(): up = lax.ppermute(up, 'item', UP)  4.38 us
    ppermute x4, starting transfers between devices, gather_columns(): far.append(lax.ppermute(pending, 'item', ACROSS))  4.32 us
  transfers between devices with their start and end apart: 23, of which 10 were waited for; matrix products, arithmetic and copies ran while one was open for 1% of the time, Pallas kernels for 20%

profile of v2, /device:TPU:1, one launch (start us, length us, event | category | flops | bytes accessed | tf_op | source)
XLA Modules:
  0.0 83.4 jit_solution(11403835713487746023)
XLA Ops:
  0.0 1.0 %constant_dynamic-update-slice_fusion.24 = (bf16[96,9216]{1,0:T(8,128)(2,1)S(1)}, bf16[128,9216]{1,0:T(8,128)(2,1)S(1)}, bf16[8,9216]{1,0:T(8,128)(2,1)S(1)}) fusion(bf16[8,3072]{1,0:T(8,128)(2,1)} %bitcast.3, bf16[8,6144]{1,0:T(8,128)(2,1)} %bitcast.2), kind=kLoop, calls=%fused_computation.30 | loop fusion | flops 294910 | bytes 589824
  1.0 2.5 %collective-permute-start = (bf16[8,9216]{1,0:T(8,128)(2,1)S(1)}, bf16[8,9216]{1,0:T(8,128)(2,1)S(1)}, u32[]{:S(2)}, u32[]{:S(2)}) collective-permute-start(bf16[8,9216]{1,0:T(8,128)(2,1)S(1)} %get-tuple-element.39), channel_id=1, source_target_pairs={{0,2},{1,3},{2,4},{3,5},{4,6},{5,7},{6,8},{7,9},{8,10},{9,11},{10,... | collective-permute-start | bytes 442376 | tf_op jit(solution)/shard_map/ppermute | solution.py:58
  3.5 4.0 %collective-permute-start.1 = (bf16[8,9216]{1,0:T(8,128)(2,1)S(1)}, bf16[8,9216]{1,0:T(8,128)(2,1)S(1)}, u32[]{:S(2)}, u32[]{:S(2)}) collective-permute-start(bf16[8,9216]{1,0:T(8,128)(2,1)S(1)} %get-tuple-element.39), channel_id=1, source_target_pairs={{0,14},{1,15},{2,0},{3,1},{4,2},{5,3},{6,4},{7,5},{8,6},{9,7},{10,... | collective-permute-start | bytes 442376 | tf_op jit(solution)/shard_map/ppermute | solution.py:57
  7.5 1.3 %collective-permute-start.6 = (bf16[8,9216]{1,0:T(8,128)(2,1)S(1)}, bf16[8,9216]{1,0:T(8,128)(2,1)S(1)}, u32[]{:S(2)}, u32[]{:S(2)}) collective-permute-start(bf16[8,9216]{1,0:T(8,128)(2,1)S(1)} %get-tuple-element.39), channel_id=1, source_target_pairs={{0,16},{1,17},{2,18},{3,19},{4,20},{5,21},{6,22},{7,23},{8,24},{9,... | collective-permute-start | bytes 442376 | tf_op jit(solution)/shard_map/ppermute | solution.py:56
  8.8 2.2 %collective-permute-done = bf16[8,9216]{1,0:T(8,128)(2,1)S(1)} collective-permute-done((bf16[8,9216]{1,0:T(8,128)(2,1)S(1)}, bf16[8,9216]{1,0:T(8,128)(2,1)S(1)}, u32[]{:S(2)}, u32[]{:S(2)}) %collective-permute-start) | collective-permute-done | bytes 147488 | tf_op jit(solution)/shard_map/ppermute | solution.py:58
  11.0 1.4 %collective-permute-start.7 = (bf16[16,9216]{1,0:T(8,128)(2,1)S(1)}, bf16[16,9216]{1,0:T(8,128)(2,1)S(1)}, u32[]{:S(2)}, u32[]{:S(2)}) collective-permute-start(bf16[16,9216]{1,0:T(8,128)(2,1)S(1)} %pad_maximum_fusion.2), channel_id=1, source_target_pairs={{0,16},{1,17},{2,18},{3,19},{4,20},{5,21},{6,22},{7,23},{8,24},{9,... | collective-permute-start | bytes 884744 | tf_op jit(solution)/shard_map/ppermute | solution.py:56
  12.4 2.7 %collective-permute-start.3 = (bf16[8,9216]{1,0:T(8,128)(2,1)S(1)}, bf16[8,9216]{1,0:T(8,128)(2,1)S(1)}, u32[]{:S(2)}, u32[]{:S(2)}) collective-permute-start(bf16[8,9216]{1,0:T(8,128)(2,1)S(1)} %collective-permute-done.1), channel_id=1, source_target_pairs={{0,14},{1,15},{2,0},{3,1},{4,2},{5,3},{6,4},{7,5},{8,6},{9,7},{10,... | collective-permute-start | bytes 442376 | tf_op jit(solution)/shard_map/ppermute | solution.py:57
  15.2 2.5 %collective-permute-done.2 = bf16[8,9216]{1,0:T(8,128)(2,1)S(1)} collective-permute-done((bf16[8,9216]{1,0:T(8,128)(2,1)S(1)}, bf16[8,9216]{1,0:T(8,128)(2,1)S(1)}, u32[]{:S(2)}, u32[]{:S(2)}) %collective-permute-start.2) | collective-permute-done | bytes 147488 | tf_op jit(solution)/shard_map/ppermute | solution.py:58
  17.7 0.3 collective-permute-start.8
  17.9 1.8 %collective-permute-start.4 = (bf16[8,9216]{1,0:T(8,128)(2,1)S(1)}, bf16[8,9216]{1,0:T(8,128)(2,1)S(1)}, u32[]{:S(2)}, u32[]{:S(2)}) collective-permute-start(bf16[8,9216]{1,0:T(8,128)(2,1)S(1)} %collective-permute-done.2), channel_id=1, source_target_pairs={{0,2},{1,3},{2,4},{3,5},{4,6},{5,7},{6,8},{7,9},{8,10},{9,11},{10,... | collective-permute-start | bytes 442376 | tf_op jit(solution)/shard_map/ppermute | solution.py:58
  19.7 0.8 %collective-permute-start.5 = (bf16[8,9216]{1,0:T(8,128)(2,1)S(1)}, bf16[8,9216]{1,0:T(8,128)(2,1)S(1)}, u32[]{:S(2)}, u32[]{:S(2)}) collective-permute-start(bf16[8,9216]{1,0:T(8,128)(2,1)S(1)} %collective-permute-done.3), channel_id=1, source_target_pairs={{0,14},{1,15},{2,0},{3,1},{4,2},{5,3},{6,4},{7,5},{8,6},{9,7},{10,... | collective-permute-start | bytes 442376 | tf_op jit(solution)/shard_map/ppermute | solution.py:57
  20.6 2.5 %collective-permute-done.4 = bf16[8,9216]{1,0:T(8,128)(2,1)S(1)} collective-permute-done((bf16[8,9216]{1,0:T(8,128)(2,1)S(1)}, bf16[8,9216]{1,0:T(8,128)(2,1)S(1)}, u32[]{:S(2)}, u32[]{:S(2)}) %collective-permute-start.4) | collective-permute-done | bytes 147488 | tf_op jit(solution)/shard_map/ppermute | solution.py:58
  23.1 0.6 collective-permute-start.9
  23.7 0.3 collective-permute-done.5
  24.0 1.8 %collective-permute-start.10 = (bf16[8,4608]{1,0:T(8,128)(2,1)S(1)}, bf16[8,4608]{1,0:T(8,128)(2,1)S(1)}, u32[]{:S(2)}, u32[]{:S(2)}) collective-permute-start(bf16[8,4608]{1,0:T(8,128)(2,1)S(1)} %slice.9), channel_id=1, source_target_pairs={{0,14},{1,15},{2,0},{3,1},{4,2},{5,3},{6,4},{7,5},{8,6},{9,7},{10,... | collective-permute-start | bytes 221192 | tf_op jit(solution)/shard_map/ppermute | solution.py:63
  26.0 1.4 %collective-permute-start.11 = (bf16[16,9216]{1,0:T(8,128)(2,1)S(1)}, bf16[16,9216]{1,0:T(8,128)(2,1)S(1)}, u32[]{:S(2)}, u32[]{:S(2)}) collective-permute-start(bf16[16,9216]{1,0:T(8,128)(2,1)S(1)} %pad_maximum_fusion.4), channel_id=1, source_target_pairs={{0,16},{1,17},{2,18},{3,19},{4,20},{5,21},{6,22},{7,23},{8,24},{9,... | collective-permute-start | bytes 884744 | tf_op jit(solution)/shard_map/ppermute | solution.py:61
  27.5 0.0 collective-permute-done.9
  27.6 0.8 collective-permute-done.10
  28.4 1.4 %collective-permute-start.12 = (bf16[8,9216]{1,0:T(8,128)(2,1)S(1)}, bf16[8,9216]{1,0:T(8,128)(2,1)S(1)}, u32[]{:S(2)}, u32[]{:S(2)}) collective-permute-start(bf16[8,9216]{1,0:T(8,128)(2,1)S(1)} %get-tuple-element.40), channel_id=1, source_target_pairs={{0,16},{1,17},{2,18},{3,19},{4,20},{5,21},{6,22},{7,23},{8,24},{9,... | collective-permute-start | bytes 442376 | tf_op jit(solution)/shard_map/ppermute | solution.py:66
  29.8 0.4 mask_users.1.refs_0_
  30.2 0.0 copy-done.1
  30.2 0.2 mask_tags.1.refs_1_
  30.5 5.7 %collective-permute-start.13 = (bf16[96,9216]{1,0:T(8,128)(2,1)S(1)}, bf16[96,9216]{1,0:T(8,128)(2,1)S(1)}, u32[]{:S(2)}, u32[]{:S(2)}) collective-permute-start(bf16[96,9216]{1,0:T(8,128)(2,1)S(1)} %get-tuple-element.19), channel_id=1, source_target_pairs={{0,1},{1,0},{2,3},{3,2},{4,5},{5,4},{6,7},{7,6},{8,9},{9,8},{10,11... | collective-permute-start | bytes 5308424 | tf_op jit(solution)/shard_map/ppermute | solution.py:284
  36.2 0.1 pad_maximum_fusion
  36.2 3.1 %collective-permute-start.14 = (bf16[32,9216]{1,0:T(8,128)(2,1)S(1)}, bf16[32,9216]{1,0:T(8,128)(2,1)S(1)}, u32[]{:S(2)}, u32[]{:S(2)}) collective-permute-start(bf16[32,9216]{1,0:T(8,128)(2,1)S(1)} %pad_maximum_fusion), channel_id=1, source_target_pairs={{0,1},{1,0},{2,3},{3,2},{4,5},{5,4},{6,7},{7,6},{8,9},{9,8},{10,11... | collective-permute-start | bytes 1769480 | tf_op jit(solution)/shard_map/ppermute | solution.py:285
  39.4 1.4 %rhs_mine.1 = f32[128,512]{1,0:T(8,128)S(1)} custom-call(bf16[128,9216]{1,0:T(8,128)(2,1)S(1)} %constant_dynamic-update-slice_fusion.2.factor_ref.mine_ref, bf16[6144,512]{1,0:T(8,128)(2,1)S(1)} %mask_users.1.refs_0_, bf16[3072,512]{1,0:T(8,128)(2,1)S(1)} %mask_tags.1.refs_1_), custom_call_target="tpu_custom_call" | custom-call | tf_op jit(solution)/shard_map/rhs_mine/pallas_call | solution.py:131
  40.8 2.6 %collective-permute-start.16 = (f32[128,512]{1,0:T(8,128)S(1)}, f32[128,512]{1,0:T(8,128)S(1)}, u32[]{:S(2)}, u32[]{:S(2)}) collective-permute-start(f32[128,512]{1,0:T(8,128)S(1)} %rhs_mine.1), channel_id=1, source_target_pairs={{0,32},{1,97},{2,34},{3,99},{4,36},{5,101},{6,38},{7,103},{8,40},{... | collective-permute-start | bytes 786440 | tf_op jit(solution)/shard_map/ppermute | solution.py:277
  43.4 0.1 constant_dynamic-update-slice_fusion.26
  43.5 1.4 %top_gram.1 = f32[128,256]{1,0:T(8,128)S(1)} custom-call(bf16[128,9216]{1,0:T(8,128)(2,1)S(1)} %constant_dynamic-update-slice_fusion.2.factor_ref.mine_ref, bf16[128,9216]{1,0:T(8,128)(2,1)S(1)} %constant_dynamic-update-slice_fusion.25.other_ref.factor_ref), custom_call_target="tpu_custom_call" | custom-call | tf_op jit(solution)/shard_map/top_gram/pallas_call | solution.py:108
  44.9 0.3 collective-permute-start.15
  45.2 1.4 %rhs_other.1 = f32[128,512]{1,0:T(8,128)S(1)} custom-call(bf16[128,9216]{1,0:T(8,128)(2,1)S(1)} %constant_dynamic-update-slice_fusion.25.other_ref.factor_ref, bf16[6144,512]{1,0:T(8,128)(2,1)S(1)} %mask_users.1.refs_0_, bf16[3072,512]{1,0:T(8,128)(2,1)S(1)} %mask_tags.1.refs_1_), custom_call_target="tpu_custom_call" | custom-call | tf_op jit(solution)/shard_map/rhs_other/pallas_call | solution.py:131
  46.6 0.0 copy-start.4
  46.6 0.0 copy-start.5
  46.6 0.7 collective-permute-done.16
  47.3 2.7 %collective-permute-done.15 = f32[128,256]{1,0:T(8,128)S(1)} collective-permute-done((f32[128,256]{1,0:T(8,128)S(1)}, f32[128,256]{1,0:T(8,128)S(1)}, u32[]{:S(2)}, u32[]{:S(2)}) %collective-permute-start.15) | collective-permute-done | bytes 131104 | tf_op jit(solution)/shard_map/ppermute | solution.py:277
  50.0 1.1 %collective-permute-start.18 = (f32[128,512]{1,0:T(8,128)S(1)}, f32[128,512]{1,0:T(8,128)S(1)}, u32[]{:S(2)}, u32[]{:S(2)}) collective-permute-start(f32[128,512]{1,0:T(8,128)S(1)} %rhs_other.1), channel_id=1, source_target_pairs={{0,32},{1,97},{2,34},{3,99},{4,36},{5,101},{6,38},{7,103},{8,40},{... | collective-permute-start | bytes 786440 | tf_op jit(solution)/shard_map/ppermute | solution.py:277
  51.2 0.1 collective-permute-start.17
  51.4 5.0 %collective-permute-done.17 = f32[128,256]{1,0:T(8,128)S(1)} collective-permute-done((f32[128,256]{1,0:T(8,128)S(1)}, f32[128,256]{1,0:T(8,128)S(1)}, u32[]{:S(2)}, u32[]{:S(2)}) %collective-permute-start.17) | collective-permute-done | bytes 131104 | tf_op jit(solution)/shard_map/ppermute | solution.py:277
  56.4 1.5 %collective-permute-done.18 = f32[128,512]{1,0:T(8,128)S(1)} collective-permute-done((f32[128,512]{1,0:T(8,128)S(1)}, f32[128,512]{1,0:T(8,128)S(1)}, u32[]{:S(2)}, u32[]{:S(2)}) %collective-permute-start.18) | collective-permute-done | bytes 262176 | tf_op jit(solution)/shard_map/ppermute | solution.py:277
  58.0 0.1 collective-permute-start.19
  58.1 0.1 add.83
  58.2 3.0 %collective-permute-start.21 = (f32[128,256]{1,0:T(8,128)S(1)}, f32[128,256]{1,0:T(8,128)S(1)}, u32[]{:S(2)}, u32[]{:S(2)}) collective-permute-start(f32[128,256]{1,0:T(8,128)S(1)} %add.86), channel_id=1, source_target_pairs={{0,128},{1,129},{2,130},{3,131},{4,132},{5,133},{6,134},{7,135},{8... | collective-permute-start | bytes 393224 | tf_op jit(solution)/shard_map/ppermute | solution.py:277
  61.2 2.4 %collective-permute-done.21 = f32[128,256]{1,0:T(8,128)S(1)} collective-permute-done((f32[128,256]{1,0:T(8,128)S(1)}, f32[128,256]{1,0:T(8,128)S(1)}, u32[]{:S(2)}, u32[]{:S(2)}) %collective-permute-start.21) | collective-permute-done | bytes 131104 | tf_op jit(solution)/shard_map/ppermute | solution.py:277
  63.6 3.3 %collective-permute-start.22 = (f32[128,256]{1,0:T(8,128)S(1)}, f32[128,256]{1,0:T(8,128)S(1)}, u32[]{:S(2)}, u32[]{:S(2)}) collective-permute-start(f32[128,256]{1,0:T(8,128)S(1)} %add.87.top_ref), channel_id=1, source_target_pairs={{0,1},{1,0},{2,3},{3,2},{4,5},{5,4},{6,7},{7,6},{8,9},{9,8},{10,11... | collective-permute-start | bytes 393224 | tf_op jit(solution)/shard_map/ppermute | solution.py:314
  67.0 0.1 fusion.7.rhs_ref
  67.0 3.2 %collective-permute-start.20 = (f32[256,512]{1,0:T(8,128)S(1)}, f32[256,512]{1,0:T(8,128)S(1)}, u32[]{:S(2)}, u32[]{:S(2)}) collective-permute-start(f32[256,512]{1,0:T(8,128)S(1)} %fusion.7.rhs_ref), channel_id=1, source_target_pairs={{0,128},{1,129},{2,130},{3,131},{4,132},{5,133},{6,134},{7,135},{8... | collective-permute-start | bytes 1572872 | tf_op jit(solution)/shard_map/ppermute | solution.py:277
  70.3 11.6 %ordered_inverse.1.inverse_ref = f32[256,256]{1,0:T(8,128)S(1)} custom-call(s32[32]{0:T(128)S(1)} %fusion.1.order_ref, f32[128,256]{1,0:T(8,128)S(1)} %add.87.top_ref, f32[128,256]{1,0:T(8,128)S(1)} %collective-permute-done.22.peer_ref), custom_call_target="tpu_custom_call" | custom-call | flops 30000001024 | bytes 100000000 | tf_op jit(solution)/shard_map/ordered_inverse/pallas_call | solution.py:242
  81.9 1.4 %final_solve.1 = f32[512,256]{1,0:T(8,128)} custom-call(f32[256,512]{1,0:T(8,128)S(1)} %fusion.7.rhs_ref, f32[256,512]{1,0:T(8,128)S(1)} %collective-permute-done.20.more_ref, f32[256,256]{1,0:T(8,128)S(1)} %ordered_inverse.1.inverse_ref), custom_call_target="tpu_custom_call" | custom-call | tf_op jit(solution)/shard_map/final_solve/pallas_call | solution.py:266
  (49 shorter events, 0.6 us)
Async XLA Ops:
  1.0 10.1 %collective-permute-start = (bf16[8,9216]{1,0:T(8,128)(2,1)S(1)}, bf16[8,9216]{1,0:T(8,128)(2,1)S(1)}, u32[]{:S(2)}, u32[]{:S(2)}) collective-permute-start(bf16[8,9216]{1,0:T(8,128)(2,1)S(1)} %get-tuple-element.39), channel_id=1, source_target_pairs={{0,2},{1,3},{2,4},{3,5},{4,6},{5,7},{6,8},{7,9},{8,10},{9,11},{10,... | collective-permute-start | bytes 442376 | tf_op jit(solution)/shard_map/ppermute | solution.py:58
  3.5 7.5 %collective-permute-start.1 = (bf16[8,9216]{1,0:T(8,128)(2,1)S(1)}, bf16[8,9216]{1,0:T(8,128)(2,1)S(1)}, u32[]{:S(2)}, u32[]{:S(2)}) collective-permute-start(bf16[8,9216]{1,0:T(8,128)(2,1)S(1)} %get-tuple-element.39), channel_id=1, source_target_pairs={{0,14},{1,15},{2,0},{3,1},{4,2},{5,3},{6,4},{7,5},{8,6},{9,7},{10,... | collective-permute-start | bytes 442376 | tf_op jit(solution)/shard_map/ppermute | solution.py:57
  7.5 18.4 %collective-permute-start.6 = (bf16[8,9216]{1,0:T(8,128)(2,1)S(1)}, bf16[8,9216]{1,0:T(8,128)(2,1)S(1)}, u32[]{:S(2)}, u32[]{:S(2)}) collective-permute-start(bf16[8,9216]{1,0:T(8,128)(2,1)S(1)} %get-tuple-element.39), channel_id=1, source_target_pairs={{0,16},{1,17},{2,18},{3,19},{4,20},{5,21},{6,22},{7,23},{8,24},{9,... | collective-permute-start | bytes 442376 | tf_op jit(solution)/shard_map/ppermute | solution.py:56
  11.0 16.4 %collective-permute-start.7 = (bf16[16,9216]{1,0:T(8,128)(2,1)S(1)}, bf16[16,9216]{1,0:T(8,128)(2,1)S(1)}, u32[]{:S(2)}, u32[]{:S(2)}) collective-permute-start(bf16[16,9216]{1,0:T(8,128)(2,1)S(1)} %pad_maximum_fusion.2), channel_id=1, source_target_pairs={{0,16},{1,17},{2,18},{3,19},{4,20},{5,21},{6,22},{7,23},{8,24},{9,... | collective-permute-start | bytes 884744 | tf_op jit(solution)/shard_map/ppermute | solution.py:56
  12.4 5.2 %collective-permute-start.2 = (bf16[8,9216]{1,0:T(8,128)(2,1)S(1)}, bf16[8,9216]{1,0:T(8,128)(2,1)S(1)}, u32[]{:S(2)}, u32[]{:S(2)}) collective-permute-start(bf16[8,9216]{1,0:T(8,128)(2,1)S(1)} %collective-permute-done), channel_id=1, source_target_pairs={{0,2},{1,3},{2,4},{3,5},{4,6},{5,7},{6,8},{7,9},{8,10},{9,11},{10,... | collective-permute-start | bytes 442376 | tf_op jit(solution)/shard_map/ppermute | solution.py:58
  12.4 5.2 %collective-permute-start.3 = (bf16[8,9216]{1,0:T(8,128)(2,1)S(1)}, bf16[8,9216]{1,0:T(8,128)(2,1)S(1)}, u32[]{:S(2)}, u32[]{:S(2)}) collective-permute-start(bf16[8,9216]{1,0:T(8,128)(2,1)S(1)} %collective-permute-done.1), channel_id=1, source_target_pairs={{0,14},{1,15},{2,0},{3,1},{4,2},{5,3},{6,4},{7,5},{8,6},{9,7},{10,... | collective-permute-start | bytes 442376 | tf_op jit(solution)/shard_map/ppermute | solution.py:57
  15.1 14.7 %copy-start.2 = (s32[48,512]{1,0:T(8,128)S(1)}, s32[48,512]{1,0:T(8,128)}, u32[]{:S(2)}) copy-start(s32[48,512]{1,0:T(8,128)} %mask_ref.2) | copy-start | bytes 294916
  15.1 14.6 %copy-start = (bf16[6144,512]{1,0:T(8,128)(2,1)S(1)}, bf16[6144,512]{1,0:T(8,128)(2,1)}, u32[]{:S(2)}) copy-start(bf16[6144,512]{1,0:T(8,128)(2,1)} %value_ref.2) | copy-start | bytes 18874372
  17.7 9.8 %collective-permute-start.8 = (bf16[16,9216]{1,0:T(8,128)(2,1)S(1)}, bf16[16,9216]{1,0:T(8,128)(2,1)S(1)}, u32[]{:S(2)}, u32[]{:S(2)}) collective-permute-start(bf16[16,9216]{1,0:T(8,128)(2,1)S(1)} %pad_maximum_fusion.3), channel_id=1, source_target_pairs={{0,16},{1,17},{2,18},{3,19},{4,20},{5,21},{6,22},{7,23},{8,24},{9,... | collective-permute-start | bytes 884744 | tf_op jit(solution)/shard_map/ppermute | solution.py:56
  17.9 5.2 %collective-permute-start.4 = (bf16[8,9216]{1,0:T(8,128)(2,1)S(1)}, bf16[8,9216]{1,0:T(8,128)(2,1)S(1)}, u32[]{:S(2)}, u32[]{:S(2)}) collective-permute-start(bf16[8,9216]{1,0:T(8,128)(2,1)S(1)} %collective-permute-done.2), channel_id=1, source_target_pairs={{0,2},{1,3},{2,4},{3,5},{4,6},{5,7},{6,8},{7,9},{8,10},{9,11},{10,... | collective-permute-start | bytes 442376 | tf_op jit(solution)/shard_map/ppermute | solution.py:58
  19.7 4.3 %collective-permute-start.5 = (bf16[8,9216]{1,0:T(8,128)(2,1)S(1)}, bf16[8,9216]{1,0:T(8,128)(2,1)S(1)}, u32[]{:S(2)}, u32[]{:S(2)}) collective-permute-start(bf16[8,9216]{1,0:T(8,128)(2,1)S(1)} %collective-permute-done.3), channel_id=1, source_target_pairs={{0,14},{1,15},{2,0},{3,1},{4,2},{5,3},{6,4},{7,5},{8,6},{9,7},{10,... | collective-permute-start | bytes 442376 | tf_op jit(solution)/shard_map/ppermute | solution.py:57
  23.1 4.4 %collective-permute-start.9 = (bf16[8,4608]{1,0:T(8,128)(2,1)S(1)}, bf16[8,4608]{1,0:T(8,128)(2,1)S(1)}, u32[]{:S(2)}, u32[]{:S(2)}) collective-permute-start(bf16[8,4608]{1,0:T(8,128)(2,1)S(1)} %slice.8), channel_id=1, source_target_pairs={{0,2},{1,3},{2,4},{3,5},{4,6},{5,7},{6,8},{7,9},{8,10},{9,11},{10,... | collective-permute-start | bytes 221192 | tf_op jit(solution)/shard_map/ppermute | solution.py:63
  24.0 4.3 %collective-permute-start.10 = (bf16[8,4608]{1,0:T(8,128)(2,1)S(1)}, bf16[8,4608]{1,0:T(8,128)(2,1)S(1)}, u32[]{:S(2)}, u32[]{:S(2)}) collective-permute-start(bf16[8,4608]{1,0:T(8,128)(2,1)S(1)} %slice.9), channel_id=1, source_target_pairs={{0,14},{1,15},{2,0},{3,1},{4,2},{5,3},{6,4},{7,5},{8,6},{9,7},{10,... | collective-permute-start | bytes 221192 | tf_op jit(solution)/shard_map/ppermute | solution.py:63
  26.0 10.2 %collective-permute-start.11 = (bf16[16,9216]{1,0:T(8,128)(2,1)S(1)}, bf16[16,9216]{1,0:T(8,128)(2,1)S(1)}, u32[]{:S(2)}, u32[]{:S(2)}) collective-permute-start(bf16[16,9216]{1,0:T(8,128)(2,1)S(1)} %pad_maximum_fusion.4), channel_id=1, source_target_pairs={{0,16},{1,17},{2,18},{3,19},{4,20},{5,21},{6,22},{7,23},{8,24},{9,... | collective-permute-start | bytes 884744 | tf_op jit(solution)/shard_map/ppermute | solution.py:61
  28.3 1.9 %copy-start.1 = (bf16[3072,512]{1,0:T(8,128)(2,1)S(1)}, bf16[3072,512]{1,0:T(8,128)(2,1)}, u32[]{:S(2)}) copy-start(bf16[3072,512]{1,0:T(8,128)(2,1)} %value_ref.3) | copy-start | bytes 9437188
  28.4 1.9 %copy-start.3 = (s32[24,512]{1,0:T(8,128)S(1)}, s32[24,512]{1,0:T(8,128)}, u32[]{:S(2)}) copy-start(s32[24,512]{1,0:T(8,128)} %mask_ref.3) | copy-start | bytes 147460
  28.4 7.8 %collective-permute-start.12 = (bf16[8,9216]{1,0:T(8,128)(2,1)S(1)}, bf16[8,9216]{1,0:T(8,128)(2,1)S(1)}, u32[]{:S(2)}, u32[]{:S(2)}) collective-permute-start(bf16[8,9216]{1,0:T(8,128)(2,1)S(1)} %get-tuple-element.40), channel_id=1, source_target_pairs={{0,16},{1,17},{2,18},{3,19},{4,20},{5,21},{6,22},{7,23},{8,24},{9,... | collective-permute-start | bytes 442376 | tf_op jit(solution)/shard_map/ppermute | solution.py:66
  30.5 12.9 %collective-permute-start.13 = (bf16[96,9216]{1,0:T(8,128)(2,1)S(1)}, bf16[96,9216]{1,0:T(8,128)(2,1)S(1)}, u32[]{:S(2)}, u32[]{:S(2)}) collective-permute-start(bf16[96,9216]{1,0:T(8,128)(2,1)S(1)} %get-tuple-element.19), channel_id=1, source_target_pairs={{0,1},{1,0},{2,3},{3,2},{4,5},{5,4},{6,7},{7,6},{8,9},{9,8},{10,11... | collective-permute-start | bytes 5308424 | tf_op jit(solution)/shard_map/ppermute | solution.py:284
  36.2 7.3 %collective-permute-start.14 = (bf16[32,9216]{1,0:T(8,128)(2,1)S(1)}, bf16[32,9216]{1,0:T(8,128)(2,1)S(1)}, u32[]{:S(2)}, u32[]{:S(2)}) collective-permute-start(bf16[32,9216]{1,0:T(8,128)(2,1)S(1)} %pad_maximum_fusion), channel_id=1, source_target_pairs={{0,1},{1,0},{2,3},{3,2},{4,5},{5,4},{6,7},{7,6},{8,9},{9,8},{10,11... | collective-permute-start | bytes 1769480 | tf_op jit(solution)/shard_map/ppermute | solution.py:285
  40.8 6.5 %collective-permute-start.16 = (f32[128,512]{1,0:T(8,128)S(1)}, f32[128,512]{1,0:T(8,128)S(1)}, u32[]{:S(2)}, u32[]{:S(2)}) collective-permute-start(f32[128,512]{1,0:T(8,128)S(1)} %rhs_mine.1), channel_id=1, source_target_pairs={{0,32},{1,97},{2,34},{3,99},{4,36},{5,101},{6,38},{7,103},{8,40},{... | collective-permute-start | bytes 786440 | tf_op jit(solution)/shard_map/ppermute | solution.py:277
  44.9 5.1 %collective-permute-start.15 = (f32[128,256]{1,0:T(8,128)S(1)}, f32[128,256]{1,0:T(8,128)S(1)}, u32[]{:S(2)}, u32[]{:S(2)}) collective-permute-start(f32[128,256]{1,0:T(8,128)S(1)} %top_gram.1), channel_id=1, source_target_pairs={{0,32},{1,97},{2,34},{3,99},{4,36},{5,101},{6,38},{7,103},{8,40},{... | collective-permute-start | bytes 393224 | tf_op jit(solution)/shard_map/ppermute | solution.py:277
  46.6 14.6 %copy-start.4 = (s32[32]{0:T(128)S(1)}, s32[32]{0:T(128)}, u32[]{:S(2)}) copy-start(s32[32]{0:T(128)} %constant.73.clone) | copy-start | bytes 388
  46.6 14.6 %copy-start.5 = (s32[32]{0:T(128)S(1)}, s32[32]{0:T(128)}, u32[]{:S(2)}) copy-start(s32[32]{0:T(128)} %constant.74.clone) | copy-start | bytes 388
  50.0 7.8 %collective-permute-start.18 = (f32[128,512]{1,0:T(8,128)S(1)}, f32[128,512]{1,0:T(8,128)S(1)}, u32[]{:S(2)}, u32[]{:S(2)}) collective-permute-start(f32[128,512]{1,0:T(8,128)S(1)} %rhs_other.1), channel_id=1, source_target_pairs={{0,32},{1,97},{2,34},{3,99},{4,36},{5,101},{6,38},{7,103},{8,40},{... | collective-permute-start | bytes 786440 | tf_op jit(solution)/shard_map/ppermute | solution.py:277
  51.2 5.2 %collective-permute-start.17 = (f32[128,256]{1,0:T(8,128)S(1)}, f32[128,256]{1,0:T(8,128)S(1)}, u32[]{:S(2)}, u32[]{:S(2)}) collective-permute-start(f32[128,256]{1,0:T(8,128)S(1)} %add.69), channel_id=1, source_target_pairs={{0,96},{1,33},{2,98},{3,35},{4,100},{5,37},{6,102},{7,39},{8,104},... | collective-permute-start | bytes 393224 | tf_op jit(solution)/shard_map/ppermute | solution.py:277
  58.0 9.0 %collective-permute-start.19 = (f32[256,512]{1,0:T(8,128)S(1)}, f32[256,512]{1,0:T(8,128)S(1)}, u32[]{:S(2)}, u32[]{:S(2)}) collective-permute-start(f32[256,512]{1,0:T(8,128)S(1)} %pad_maximum_fusion.1), channel_id=1, source_target_pairs={{0,96},{1,33},{2,98},{3,35},{4,100},{5,37},{6,102},{7,39},{8,104},... | collective-permute-start | bytes 1572872 | tf_op jit(solution)/shard_map/ppermute | solution.py:277
  58.2 5.4 %collective-permute-start.21 = (f32[128,256]{1,0:T(8,128)S(1)}, f32[128,256]{1,0:T(8,128)S(1)}, u32[]{:S(2)}, u32[]{:S(2)}) collective-permute-start(f32[128,256]{1,0:T(8,128)S(1)} %add.86), channel_id=1, source_target_pairs={{0,128},{1,129},{2,130},{3,131},{4,132},{5,133},{6,134},{7,135},{8... | collective-permute-start | bytes 393224 | tf_op jit(solution)/shard_map/ppermute | solution.py:277
  63.6 6.6 %collective-permute-start.22 = (f32[128,256]{1,0:T(8,128)S(1)}, f32[128,256]{1,0:T(8,128)S(1)}, u32[]{:S(2)}, u32[]{:S(2)}) collective-permute-start(f32[128,256]{1,0:T(8,128)S(1)} %add.87.top_ref), channel_id=1, source_target_pairs={{0,1},{1,0},{2,3},{3,2},{4,5},{5,4},{6,7},{7,6},{8,9},{9,8},{10,11... | collective-permute-start | bytes 393224 | tf_op jit(solution)/shard_map/ppermute | solution.py:314
  67.0 14.9 %collective-permute-start.20 = (f32[256,512]{1,0:T(8,128)S(1)}, f32[256,512]{1,0:T(8,128)S(1)}, u32[]{:S(2)}, u32[]{:S(2)}) collective-permute-start(f32[256,512]{1,0:T(8,128)S(1)} %fusion.7.rhs_ref), channel_id=1, source_target_pairs={{0,128},{1,129},{2,130},{3,131},{4,132},{5,133},{6,134},{7,135},{8... | collective-permute-start | bytes 1572872 | tf_op jit(solution)/shard_map/ppermute | solution.py:277

commit v3 on v2

--- a/solution.py
+++ b/solution.py
@@ -10,7 +10,7 @@
 LAMBDA = 0.5
 REG = 0.1
 SUB = 8
-BLOCK = 32
+BLOCK = 16
 
 NY, NZ, NC = 2, 8, 2
 NYH, NX = 2, 4
@@ -213,6 +213,19 @@
                     panel[i][s] = old - weighted_rows(left, rows[s])
         block = jnp.concatenate([jnp.concatenate(panel[q], axis=1) for q in range(panels)], axis=0)
         r1 = r0 + BLOCK
+        inside = (wide >= base) & (wide < base + BLOCK)
+
+        def update(low, high):
+            change = jnp.dot(
+                a_ref[low:high, r0:r1], block, preferred_element_type=jnp.float32, precision=lax.Precision.HIGHEST
+            )
+            for s in range(2):
+                at = slice(s * 128, (s + 1) * 128)
+                old = a_ref[low:high, at]
+                if s == side:
+                    old = jnp.where(inside, 0.0, old)
+                a_ref[low:high, at] = old - change[:, at]
+
         if r1 < n:
             left = [spread(a_ref[r1 : r1 + SUB, r0 + m : r0 + m + 1]) for m in range(BLOCK)]
             ahead = []
@@ -220,17 +233,17 @@
                 old = a_ref[r1 : r1 + SUB, s * 128 : (s + 1) * 128]
                 if s == side:
                     old = jnp.where((lane >= base) & (lane < base + BLOCK), 0.0, old)
+                change = None
                 for q in range(panels):
                     rows = [spread(panel[q][s][m : m + 1, :]) for m in range(SUB)]
-                    old = old - weighted_rows(left[q * SUB : (q + 1) * SUB], rows)
-                ahead.append(old)
-        change = jnp.dot(a_ref[:, r0:r1], block, preferred_element_type=jnp.float32, precision=lax.Precision.HIGHEST)
-        for s in range(2):
-            at = slice(s * 128, (s + 1) * 128)
-            old = a_ref[:, at]
-            if s == side:
-                old = jnp.where((wide >= base) & (wide < base + BLOCK), 0.0, old)
-            a_ref[:, at] = old - change[:, at]
+                    part = weighted_rows(left[q * SUB : (q + 1) * SUB], rows)
+                    change = part if change is None else change + part
+                ahead.append(old - change)
+            update(r1, r1 + BLOCK)
+            if r1 + BLOCK < n:
+                update(r1 + BLOCK, n)
+        if r0 > 0:
+            update(0, r0)
         a_ref[r0:r1, :] = block
 
     for b in range(n // 8):
@@ -246,7 +259,7 @@
         out_specs=whole(),
         scratch_shapes=[pltpu.VMEM((n, n), jnp.float32)],
         compiler_params=pltpu.CompilerParams(vmem_limit_bytes=4 << 20),
-        cost_estimate=pl.CostEstimate(flops=3 * 10**10, bytes_accessed=10**8, transcendentals=0),
+        cost_estimate=pl.CostEstimate(flops=2 * 10**9, bytes_accessed=0, transcendentals=0),
         name="ordered_inverse",
     )(order, top, peer)
 
@@ -303,14 +316,12 @@
     top, later = lax.optimization_barrier((top, other))
     rhs_other = rhs_rows(later, parts, "rhs_other")
 
-    fresh, peer_mine, rhs_other = lax.optimization_barrier((swap(top, 0), swap(rhs_mine, 0), rhs_other))
+    fresh, peer_mine, peer_other = lax.optimization_barrier((swap(top, 0), swap(rhs_mine, 0), swap(rhs_other, 0)))
     top = top + fresh
-    rhs_mine = rhs_mine + peer_mine
-    fresh, peer_other = lax.optimization_barrier((swap(top, 1), swap(rhs_other, 0)))
-    top = top + fresh
-    rhs = jnp.concatenate([rhs_mine, rhs_other + peer_other], axis=0)
+    rhs = jnp.concatenate([rhs_mine + peer_mine, rhs_other + peer_other], axis=0)
+    top = top + swap(top, 2)
     rhs = rhs + swap(rhs, 1)
-    top = top + swap(top, 2)
+    top = top + swap(top, 1)
     inverse = ordered_inverse(order, top, lax.ppermute(top, "item", CORE))
     return final_solve(rhs, swap(rhs, 2), inverse)
 

time: 83.7 us -> 80.1 us (0.957)
  waiting for transfers between devices: 20.6 us -> 16.8 us
  starting transfers between devices: 42.6 us -> 45.9 us
  Pallas kernels: 17.9 us -> 15.1 us
    ppermute x7, waiting for transfers between devices: 12.3 us -> 7.59 us  [swap(): return lax.ppermute(value, ('band', 'item'), band_perm(stage))]
    ppermute x7, starting transfers between devices: 10.4 us -> 14.4 us  [swap(): return lax.ppermute(value, ('band', 'item'), band_perm(stage))]
    pallas_call x1, Pallas kernels: 11.6 us -> 8.83 us  [ordered_inverse(): pl.pallas_call(inverse_kernel, out_shape=jax.ShapeDtypeStruct((n, n), jnp...]
    ppermute x1, waiting for transfers between devices: 0.01 us -> 0.96 us  [body(): inverse = ordered_inverse(order, top, lax.ppermute(top, 'item', CORE))]
  transfers between devices with their start and end apart: 23 -> 23, of which waited for: 10 -> 8; matrix products, arithmetic and copies ran while one was open for 1% -> 1% of each run, Pallas kernels for 20% -> 17%
where the time goes in v3:
time: 80.1 us; the launch traced here: 80 us
  starting transfers between devices  45.9 us (57%)
  waiting for transfers between devices  16.8 us (21%)
  Pallas kernels  15.1 us (19%)
  other arithmetic  1.33 us (2%)
    ppermute x7, starting transfers between devices, swap(): return lax.ppermute(value, ('band', 'item'), band_perm(stage))  14.4 us
    pallas_call x1, Pallas kernels, ordered_inverse(): pl.pallas_call(inverse_kernel, out_shape=jax.ShapeDtypeStruct((n, n), jnp...  8.83 us
    ppermute x7, waiting for transfers between devices, swap(): return lax.ppermute(value, ('band', 'item'), band_perm(stage))  7.59 us
    ppermute x3, starting transfers between devices, gather_columns(): down = lax.ppermute(down, 'item', DOWN)  7.55 us
    ppermute x3, waiting for transfers between devices, gather_columns(): up = lax.ppermute(up, 'item', UP)  7.12 us
    ppermute x1, starting transfers between devices, body(): other_first = lax.ppermute(first, 'item', CORE)  5.69 us
    ppermute x3, starting transfers between devices, gather_columns(): up = lax.ppermute(up, 'item', UP)  4.38 us
    ppermute x4, starting transfers between devices, gather_columns(): far.append(lax.ppermute(pending, 'item', ACROSS))  4.32 us
  transfers between devices with their start and end apart: 23, of which 8 were waited for; matrix products, arithmetic and copies ran while one was open for 1% of the time, Pallas kernels for 17%

profile of v3, /device:TPU:1, one launch (start us, length us, event | category | flops | bytes accessed | tf_op | source)
XLA Modules:
  0.0 80.0 jit_solution(7077925865257402488)
XLA Ops:
  0.0 1.0 %constant_dynamic-update-slice_fusion.24 = (bf16[96,9216]{1,0:T(8,128)(2,1)S(1)}, bf16[128,9216]{1,0:T(8,128)(2,1)S(1)}, bf16[8,9216]{1,0:T(8,128)(2,1)S(1)}) fusion(bf16[8,3072]{1,0:T(8,128)(2,1)} %bitcast.3, bf16[8,6144]{1,0:T(8,128)(2,1)} %bitcast.2), kind=kLoop, calls=%fused_computation.30 | loop fusion | flops 294910 | bytes 589824
  1.0 2.5 %collective-permute-start = (bf16[8,9216]{1,0:T(8,128)(2,1)S(1)}, bf16[8,9216]{1,0:T(8,128)(2,1)S(1)}, u32[]{:S(2)}, u32[]{:S(2)}) collective-permute-start(bf16[8,9216]{1,0:T(8,128)(2,1)S(1)} %get-tuple-element.35), channel_id=1, source_target_pairs={{0,2},{1,3},{2,4},{3,5},{4,6},{5,7},{6,8},{7,9},{8,10},{9,11},{10,... | collective-permute-start | bytes 442376 | tf_op jit(solution)/shard_map/ppermute | solution.py:58
  3.5 4.0 %collective-permute-start.1 = (bf16[8,9216]{1,0:T(8,128)(2,1)S(1)}, bf16[8,9216]{1,0:T(8,128)(2,1)S(1)}, u32[]{:S(2)}, u32[]{:S(2)}) collective-permute-start(bf16[8,9216]{1,0:T(8,128)(2,1)S(1)} %get-tuple-element.35), channel_id=1, source_target_pairs={{0,14},{1,15},{2,0},{3,1},{4,2},{5,3},{6,4},{7,5},{8,6},{9,7},{10,... | collective-permute-start | bytes 442376 | tf_op jit(solution)/shard_map/ppermute | solution.py:57
  7.5 1.3 %collective-permute-start.6 = (bf16[8,9216]{1,0:T(8,128)(2,1)S(1)}, bf16[8,9216]{1,0:T(8,128)(2,1)S(1)}, u32[]{:S(2)}, u32[]{:S(2)}) collective-permute-start(bf16[8,9216]{1,0:T(8,128)(2,1)S(1)} %get-tuple-element.35), channel_id=1, source_target_pairs={{0,16},{1,17},{2,18},{3,19},{4,20},{5,21},{6,22},{7,23},{8,24},{9,... | collective-permute-start | bytes 442376 | tf_op jit(solution)/shard_map/ppermute | solution.py:56
  8.8 2.2 %collective-permute-done = bf16[8,9216]{1,0:T(8,128)(2,1)S(1)} collective-permute-done((bf16[8,9216]{1,0:T(8,128)(2,1)S(1)}, bf16[8,9216]{1,0:T(8,128)(2,1)S(1)}, u32[]{:S(2)}, u32[]{:S(2)}) %collective-permute-start) | collective-permute-done | bytes 147488 | tf_op jit(solution)/shard_map/ppermute | solution.py:58
  11.0 1.4 %collective-permute-start.7 = (bf16[16,9216]{1,0:T(8,128)(2,1)S(1)}, bf16[16,9216]{1,0:T(8,128)(2,1)S(1)}, u32[]{:S(2)}, u32[]{:S(2)}) collective-permute-start(bf16[16,9216]{1,0:T(8,128)(2,1)S(1)} %pad_maximum_fusion.2), channel_id=1, source_target_pairs={{0,16},{1,17},{2,18},{3,19},{4,20},{5,21},{6,22},{7,23},{8,24},{9,... | collective-permute-start | bytes 884744 | tf_op jit(solution)/shard_map/ppermute | solution.py:56
  12.4 2.7 %collective-permute-start.3 = (bf16[8,9216]{1,0:T(8,128)(2,1)S(1)}, bf16[8,9216]{1,0:T(8,128)(2,1)S(1)}, u32[]{:S(2)}, u32[]{:S(2)}) collective-permute-start(bf16[8,9216]{1,0:T(8,128)(2,1)S(1)} %collective-permute-done.1), channel_id=1, source_target_pairs={{0,14},{1,15},{2,0},{3,1},{4,2},{5,3},{6,4},{7,5},{8,6},{9,7},{10,... | collective-permute-start | bytes 442376 | tf_op jit(solution)/shard_map/ppermute | solution.py:57
  15.1 0.0 copy-start
  15.2 2.5 %collective-permute-done.2 = bf16[8,9216]{1,0:T(8,128)(2,1)S(1)} collective-permute-done((bf16[8,9216]{1,0:T(8,128)(2,1)S(1)}, bf16[8,9216]{1,0:T(8,128)(2,1)S(1)}, u32[]{:S(2)}, u32[]{:S(2)}) %collective-permute-start.2) | collective-permute-done | bytes 147488 | tf_op jit(solution)/shard_map/ppermute | solution.py:58
  17.7 0.3 collective-permute-start.8
  17.9 1.8 %collective-permute-start.4 = (bf16[8,9216]{1,0:T(8,128)(2,1)S(1)}, bf16[8,9216]{1,0:T(8,128)(2,1)S(1)}, u32[]{:S(2)}, u32[]{:S(2)}) collective-permute-start(bf16[8,9216]{1,0:T(8,128)(2,1)S(1)} %collective-permute-done.2), channel_id=1, source_target_pairs={{0,2},{1,3},{2,4},{3,5},{4,6},{5,7},{6,8},{7,9},{8,10},{9,11},{10,... | collective-permute-start | bytes 442376 | tf_op jit(solution)/shard_map/ppermute | solution.py:58
  19.7 0.8 %collective-permute-start.5 = (bf16[8,9216]{1,0:T(8,128)(2,1)S(1)}, bf16[8,9216]{1,0:T(8,128)(2,1)S(1)}, u32[]{:S(2)}, u32[]{:S(2)}) collective-permute-start(bf16[8,9216]{1,0:T(8,128)(2,1)S(1)} %collective-permute-done.3), channel_id=1, source_target_pairs={{0,14},{1,15},{2,0},{3,1},{4,2},{5,3},{6,4},{7,5},{8,6},{9,7},{10,... | collective-permute-start | bytes 442376 | tf_op jit(solution)/shard_map/ppermute | solution.py:57
  20.6 2.5 %collective-permute-done.4 = bf16[8,9216]{1,0:T(8,128)(2,1)S(1)} collective-permute-done((bf16[8,9216]{1,0:T(8,128)(2,1)S(1)}, bf16[8,9216]{1,0:T(8,128)(2,1)S(1)}, u32[]{:S(2)}, u32[]{:S(2)}) %collective-permute-start.4) | collective-permute-done | bytes 147488 | tf_op jit(solution)/shard_map/ppermute | solution.py:58
  23.1 0.6 collective-permute-start.9
  23.7 0.3 collective-permute-done.5
  24.0 1.8 %collective-permute-start.10 = (bf16[8,4608]{1,0:T(8,128)(2,1)S(1)}, bf16[8,4608]{1,0:T(8,128)(2,1)S(1)}, u32[]{:S(2)}, u32[]{:S(2)}) collective-permute-start(bf16[8,4608]{1,0:T(8,128)(2,1)S(1)} %slice.9), channel_id=1, source_target_pairs={{0,14},{1,15},{2,0},{3,1},{4,2},{5,3},{6,4},{7,5},{8,6},{9,7},{10,... | collective-permute-start | bytes 221192 | tf_op jit(solution)/shard_map/ppermute | solution.py:63
  26.0 1.4 %collective-permute-start.11 = (bf16[16,9216]{1,0:T(8,128)(2,1)S(1)}, bf16[16,9216]{1,0:T(8,128)(2,1)S(1)}, u32[]{:S(2)}, u32[]{:S(2)}) collective-permute-start(bf16[16,9216]{1,0:T(8,128)(2,1)S(1)} %pad_maximum_fusion.4), channel_id=1, source_target_pairs={{0,16},{1,17},{2,18},{3,19},{4,20},{5,21},{6,22},{7,23},{8,24},{9,... | collective-permute-start | bytes 884744 | tf_op jit(solution)/shard_map/ppermute | solution.py:61
  27.5 0.0 collective-permute-done.9
  27.6 0.8 collective-permute-done.10
  28.3 0.0 copy-start.1
  28.4 1.4 %collective-permute-start.12 = (bf16[8,9216]{1,0:T(8,128)(2,1)S(1)}, bf16[8,9216]{1,0:T(8,128)(2,1)S(1)}, u32[]{:S(2)}, u32[]{:S(2)}) collective-permute-start(bf16[8,9216]{1,0:T(8,128)(2,1)S(1)} %get-tuple-element.36), channel_id=1, source_target_pairs={{0,16},{1,17},{2,18},{3,19},{4,20},{5,21},{6,22},{7,23},{8,24},{9,... | collective-permute-start | bytes 442376 | tf_op jit(solution)/shard_map/ppermute | solution.py:66
  29.8 0.4 mask_users.1.refs_0_
  30.2 0.0 copy-done.1
  30.2 0.2 mask_tags.1.refs_1_
  30.5 5.7 %collective-permute-start.13 = (bf16[96,9216]{1,0:T(8,128)(2,1)S(1)}, bf16[96,9216]{1,0:T(8,128)(2,1)S(1)}, u32[]{:S(2)}, u32[]{:S(2)}) collective-permute-start(bf16[96,9216]{1,0:T(8,128)(2,1)S(1)} %get-tuple-element.15), channel_id=1, source_target_pairs={{0,1},{1,0},{2,3},{3,2},{4,5},{5,4},{6,7},{7,6},{8,9},{9,8},{10,11... | collective-permute-start | bytes 5308424 | tf_op jit(solution)/shard_map/ppermute | solution.py:297
  36.2 0.1 pad_maximum_fusion
  36.2 3.1 %collective-permute-start.14 = (bf16[32,9216]{1,0:T(8,128)(2,1)S(1)}, bf16[32,9216]{1,0:T(8,128)(2,1)S(1)}, u32[]{:S(2)}, u32[]{:S(2)}) collective-permute-start(bf16[32,9216]{1,0:T(8,128)(2,1)S(1)} %pad_maximum_fusion), channel_id=1, source_target_pairs={{0,1},{1,0},{2,3},{3,2},{4,5},{5,4},{6,7},{7,6},{8,9},{9,8},{10,11... | collective-permute-start | bytes 1769480 | tf_op jit(solution)/shard_map/ppermute | solution.py:298
  39.4 1.4 %rhs_mine.1 = f32[128,512]{1,0:T(8,128)S(1)} custom-call(bf16[128,9216]{1,0:T(8,128)(2,1)S(1)} %constant_dynamic-update-slice_fusion.2.factor_ref.mine_ref, bf16[6144,512]{1,0:T(8,128)(2,1)S(1)} %mask_users.1.refs_0_, bf16[3072,512]{1,0:T(8,128)(2,1)S(1)} %mask_tags.1.refs_1_), custom_call_target="tpu_custom_call" | custom-call | tf_op jit(solution)/shard_map/rhs_mine/pallas_call | solution.py:131
  40.8 2.6 %collective-permute-start.16 = (f32[128,512]{1,0:T(8,128)S(1)}, f32[128,512]{1,0:T(8,128)S(1)}, u32[]{:S(2)}, u32[]{:S(2)}) collective-permute-start(f32[128,512]{1,0:T(8,128)S(1)} %rhs_mine.1), channel_id=1, source_target_pairs={{0,32},{1,97},{2,34},{3,99},{4,36},{5,101},{6,38},{7,103},{8,40},{... | collective-permute-start | bytes 786440 | tf_op jit(solution)/shard_map/ppermute | solution.py:290
  43.4 0.1 constant_dynamic-update-slice_fusion.26
  43.5 1.4 %top_gram.1 = f32[128,256]{1,0:T(8,128)S(1)} custom-call(bf16[128,9216]{1,0:T(8,128)(2,1)S(1)} %constant_dynamic-update-slice_fusion.2.factor_ref.mine_ref, bf16[128,9216]{1,0:T(8,128)(2,1)S(1)} %constant_dynamic-update-slice_fusion.25.other_ref.factor_ref), custom_call_target="tpu_custom_call" | custom-call | tf_op jit(solution)/shard_map/top_gram/pallas_call | solution.py:108
  44.9 1.4 %rhs_other.1 = f32[128,512]{1,0:T(8,128)S(1)} custom-call(bf16[128,9216]{1,0:T(8,128)(2,1)S(1)} %constant_dynamic-update-slice_fusion.25.other_ref.factor_ref, bf16[6144,512]{1,0:T(8,128)(2,1)S(1)} %mask_users.1.refs_0_, bf16[3072,512]{1,0:T(8,128)(2,1)S(1)} %mask_tags.1.refs_1_), custom_call_target="tpu_custom_call" | custom-call | tf_op jit(solution)/shard_map/rhs_other/pallas_call | solution.py:131
  46.3 0.3 collective-permute-start.17
  46.6 2.5 %collective-permute-start.15 = (f32[128,256]{1,0:T(8,128)S(1)}, f32[128,256]{1,0:T(8,128)S(1)}, u32[]{:S(2)}, u32[]{:S(2)}) collective-permute-start(f32[128,256]{1,0:T(8,128)S(1)} %top_gram.1), channel_id=1, source_target_pairs={{0,32},{1,97},{2,34},{3,99},{4,36},{5,101},{6,38},{7,103},{8,40},{... | collective-permute-start | bytes 393224 | tf_op jit(solution)/shard_map/ppermute | solution.py:290
  49.1 5.2 %collective-permute-done.15 = f32[128,256]{1,0:T(8,128)S(1)} collective-permute-done((f32[128,256]{1,0:T(8,128)S(1)}, f32[128,256]{1,0:T(8,128)S(1)}, u32[]{:S(2)}, u32[]{:S(2)}) %collective-permute-start.15) | collective-permute-done | bytes 131104 | tf_op jit(solution)/shard_map/ppermute | solution.py:290
  54.3 0.0 copy-start.4
  54.3 0.0 copy-start.5
  54.4 0.1 collective-permute-start.18
  54.5 3.0 %collective-permute-start.20 = (f32[128,256]{1,0:T(8,128)S(1)}, f32[128,256]{1,0:T(8,128)S(1)}, u32[]{:S(2)}, u32[]{:S(2)}) collective-permute-start(f32[128,256]{1,0:T(8,128)S(1)} %add.85), channel_id=1, source_target_pairs={{0,128},{1,129},{2,130},{3,131},{4,132},{5,133},{6,134},{7,135},{8... | collective-permute-start | bytes 393224 | tf_op jit(solution)/shard_map/ppermute | solution.py:290
  57.5 2.4 %collective-permute-done.20 = f32[128,256]{1,0:T(8,128)S(1)} collective-permute-done((f32[128,256]{1,0:T(8,128)S(1)}, f32[128,256]{1,0:T(8,128)S(1)}, u32[]{:S(2)}, u32[]{:S(2)}) %collective-permute-start.20) | collective-permute-done | bytes 131104 | tf_op jit(solution)/shard_map/ppermute | solution.py:290
  60.0 2.9 %collective-permute-start.21 = (f32[128,256]{1,0:T(8,128)S(1)}, f32[128,256]{1,0:T(8,128)S(1)}, u32[]{:S(2)}, u32[]{:S(2)}) collective-permute-start(f32[128,256]{1,0:T(8,128)S(1)} %add.86), channel_id=1, source_target_pairs={{0,96},{1,33},{2,98},{3,35},{4,100},{5,37},{6,102},{7,39},{8,104},... | collective-permute-start | bytes 393224 | tf_op jit(solution)/shard_map/ppermute | solution.py:290
  62.9 0.1 fusion.7.rhs_ref
  63.0 3.0 %collective-permute-start.19 = (f32[256,512]{1,0:T(8,128)S(1)}, f32[256,512]{1,0:T(8,128)S(1)}, u32[]{:S(2)}, u32[]{:S(2)}) collective-permute-start(f32[256,512]{1,0:T(8,128)S(1)} %fusion.7.rhs_ref), channel_id=1, source_target_pairs={{0,128},{1,129},{2,130},{3,131},{4,132},{5,133},{6,134},{7,135},{8... | collective-permute-start | bytes 1572872 | tf_op jit(solution)/shard_map/ppermute | solution.py:290
  66.0 0.1 add.82
  66.1 2.7 %collective-permute-start.22 = (f32[128,256]{1,0:T(8,128)S(1)}, f32[128,256]{1,0:T(8,128)S(1)}, u32[]{:S(2)}, u32[]{:S(2)}) collective-permute-start(f32[128,256]{1,0:T(8,128)S(1)} %add.87.top_ref), channel_id=1, source_target_pairs={{0,1},{1,0},{2,3},{3,2},{4,5},{5,4},{6,7},{7,6},{8,9},{9,8},{10,11... | collective-permute-start | bytes 393224 | tf_op jit(solution)/shard_map/ppermute | solution.py:325
  68.8 1.0 %collective-permute-done.22.peer_ref = f32[128,256]{1,0:T(8,128)S(1)} collective-permute-done((f32[128,256]{1,0:T(8,128)S(1)}, f32[128,256]{1,0:T(8,128)S(1)}, u32[]{:S(2)}, u32[]{:S(2)}) %collective-permute-start.22) | collective-permute-done | bytes 131104 | tf_op jit(solution)/shard_map/ppermute | solution.py:325
  69.7 8.8 %ordered_inverse.1.inverse_ref = f32[256,256]{1,0:T(8,128)S(1)} custom-call(s32[32]{0:T(128)S(1)} %fusion.1.order_ref, f32[128,256]{1,0:T(8,128)S(1)} %add.87.top_ref, f32[128,256]{1,0:T(8,128)S(1)} %collective-permute-done.22.peer_ref), custom_call_target="tpu_custom_call" | custom-call | flops 2000000000 | tf_op jit(solution)/shard_map/ordered_inverse/pallas_call | solution.py:255
  78.6 1.4 %final_solve.1 = f32[512,256]{1,0:T(8,128)} custom-call(f32[256,512]{1,0:T(8,128)S(1)} %fusion.7.rhs_ref, f32[256,512]{1,0:T(8,128)S(1)} %collective-permute-done.19.more_ref, f32[256,256]{1,0:T(8,128)S(1)} %ordered_inverse.1.inverse_ref), custom_call_target="tpu_custom_call" | custom-call | tf_op jit(solution)/shard_map/final_solve/pallas_call | solution.py:279
  (49 shorter events, 0.6 us)
Async XLA Ops:
  1.0 10.1 %collective-permute-start = (bf16[8,9216]{1,0:T(8,128)(2,1)S(1)}, bf16[8,9216]{1,0:T(8,128)(2,1)S(1)}, u32[]{:S(2)}, u32[]{:S(2)}) collective-permute-start(bf16[8,9216]{1,0:T(8,128)(2,1)S(1)} %get-tuple-element.35), channel_id=1, source_target_pairs={{0,2},{1,3},{2,4},{3,5},{4,6},{5,7},{6,8},{7,9},{8,10},{9,11},{10,... | collective-permute-start | bytes 442376 | tf_op jit(solution)/shard_map/ppermute | solution.py:58
  3.5 7.5 %collective-permute-start.1 = (bf16[8,9216]{1,0:T(8,128)(2,1)S(1)}, bf16[8,9216]{1,0:T(8,128)(2,1)S(1)}, u32[]{:S(2)}, u32[]{:S(2)}) collective-permute-start(bf16[8,9216]{1,0:T(8,128)(2,1)S(1)} %get-tuple-element.35), channel_id=1, source_target_pairs={{0,14},{1,15},{2,0},{3,1},{4,2},{5,3},{6,4},{7,5},{8,6},{9,7},{10,... | collective-permute-start | bytes 442376 | tf_op jit(solution)/shard_map/ppermute | solution.py:57
  7.5 18.4 %collective-permute-start.6 = (bf16[8,9216]{1,0:T(8,128)(2,1)S(1)}, bf16[8,9216]{1,0:T(8,128)(2,1)S(1)}, u32[]{:S(2)}, u32[]{:S(2)}) collective-permute-start(bf16[8,9216]{1,0:T(8,128)(2,1)S(1)} %get-tuple-element.35), channel_id=1, source_target_pairs={{0,16},{1,17},{2,18},{3,19},{4,20},{5,21},{6,22},{7,23},{8,24},{9,... | collective-permute-start | bytes 442376 | tf_op jit(solution)/shard_map/ppermute | solution.py:56
  11.0 16.4 %collective-permute-start.7 = (bf16[16,9216]{1,0:T(8,128)(2,1)S(1)}, bf16[16,9216]{1,0:T(8,128)(2,1)S(1)}, u32[]{:S(2)}, u32[]{:S(2)}) collective-permute-start(bf16[16,9216]{1,0:T(8,128)(2,1)S(1)} %pad_maximum_fusion.2), channel_id=1, source_target_pairs={{0,16},{1,17},{2,18},{3,19},{4,20},{5,21},{6,22},{7,23},{8,24},{9,... | collective-permute-start | bytes 884744 | tf_op jit(solution)/shard_map/ppermute | solution.py:56
  12.4 5.2 %collective-permute-start.2 = (bf16[8,9216]{1,0:T(8,128)(2,1)S(1)}, bf16[8,9216]{1,0:T(8,128)(2,1)S(1)}, u32[]{:S(2)}, u32[]{:S(2)}) collective-permute-start(bf16[8,9216]{1,0:T(8,128)(2,1)S(1)} %collective-permute-done), channel_id=1, source_target_pairs={{0,2},{1,3},{2,4},{3,5},{4,6},{5,7},{6,8},{7,9},{8,10},{9,11},{10,... | collective-permute-start | bytes 442376 | tf_op jit(solution)/shard_map/ppermute | solution.py:58
  12.4 5.2 %collective-permute-start.3 = (bf16[8,9216]{1,0:T(8,128)(2,1)S(1)}, bf16[8,9216]{1,0:T(8,128)(2,1)S(1)}, u32[]{:S(2)}, u32[]{:S(2)}) collective-permute-start(bf16[8,9216]{1,0:T(8,128)(2,1)S(1)} %collective-permute-done.1), channel_id=1, source_target_pairs={{0,14},{1,15},{2,0},{3,1},{4,2},{5,3},{6,4},{7,5},{8,6},{9,7},{10,... | collective-permute-start | bytes 442376 | tf_op jit(solution)/shard_map/ppermute | solution.py:57
  15.1 14.7 %copy-start.2 = (s32[48,512]{1,0:T(8,128)S(1)}, s32[48,512]{1,0:T(8,128)}, u32[]{:S(2)}) copy-start(s32[48,512]{1,0:T(8,128)} %mask_ref.2) | copy-start | bytes 294916
  15.1 14.6 %copy-start = (bf16[6144,512]{1,0:T(8,128)(2,1)S(1)}, bf16[6144,512]{1,0:T(8,128)(2,1)}, u32[]{:S(2)}) copy-start(bf16[6144,512]{1,0:T(8,128)(2,1)} %value_ref.2) | copy-start | bytes 18874372
  17.7 9.8 %collective-permute-start.8 = (bf16[16,9216]{1,0:T(8,128)(2,1)S(1)}, bf16[16,9216]{1,0:T(8,128)(2,1)S(1)}, u32[]{:S(2)}, u32[]{:S(2)}) collective-permute-start(bf16[16,9216]{1,0:T(8,128)(2,1)S(1)} %pad_maximum_fusion.3), channel_id=1, source_target_pairs={{0,16},{1,17},{2,18},{3,19},{4,20},{5,21},{6,22},{7,23},{8,24},{9,... | collective-permute-start | bytes 884744 | tf_op jit(solution)/shard_map/ppermute | solution.py:56
  17.9 5.2 %collective-permute-start.4 = (bf16[8,9216]{1,0:T(8,128)(2,1)S(1)}, bf16[8,9216]{1,0:T(8,128)(2,1)S(1)}, u32[]{:S(2)}, u32[]{:S(2)}) collective-permute-start(bf16[8,9216]{1,0:T(8,128)(2,1)S(1)} %collective-permute-done.2), channel_id=1, source_target_pairs={{0,2},{1,3},{2,4},{3,5},{4,6},{5,7},{6,8},{7,9},{8,10},{9,11},{10,... | collective-permute-start | bytes 442376 | tf_op jit(solution)/shard_map/ppermute | solution.py:58
  19.7 4.3 %collective-permute-start.5 = (bf16[8,9216]{1,0:T(8,128)(2,1)S(1)}, bf16[8,9216]{1,0:T(8,128)(2,1)S(1)}, u32[]{:S(2)}, u32[]{:S(2)}) collective-permute-start(bf16[8,9216]{1,0:T(8,128)(2,1)S(1)} %collective-permute-done.3), channel_id=1, source_target_pairs={{0,14},{1,15},{2,0},{3,1},{4,2},{5,3},{6,4},{7,5},{8,6},{9,7},{10,... | collective-permute-start | bytes 442376 | tf_op jit(solution)/shard_map/ppermute | solution.py:57
  23.1 4.4 %collective-permute-start.9 = (bf16[8,4608]{1,0:T(8,128)(2,1)S(1)}, bf16[8,4608]{1,0:T(8,128)(2,1)S(1)}, u32[]{:S(2)}, u32[]{:S(2)}) collective-permute-start(bf16[8,4608]{1,0:T(8,128)(2,1)S(1)} %slice.8), channel_id=1, source_target_pairs={{0,2},{1,3},{2,4},{3,5},{4,6},{5,7},{6,8},{7,9},{8,10},{9,11},{10,... | collective-permute-start | bytes 221192 | tf_op jit(solution)/shard_map/ppermute | solution.py:63
  24.0 4.3 %collective-permute-start.10 = (bf16[8,4608]{1,0:T(8,128)(2,1)S(1)}, bf16[8,4608]{1,0:T(8,128)(2,1)S(1)}, u32[]{:S(2)}, u32[]{:S(2)}) collective-permute-start(bf16[8,4608]{1,0:T(8,128)(2,1)S(1)} %slice.9), channel_id=1, source_target_pairs={{0,14},{1,15},{2,0},{3,1},{4,2},{5,3},{6,4},{7,5},{8,6},{9,7},{10,... | collective-permute-start | bytes 221192 | tf_op jit(solution)/shard_map/ppermute | solution.py:63
  26.0 10.2 %collective-permute-start.11 = (bf16[16,9216]{1,0:T(8,128)(2,1)S(1)}, bf16[16,9216]{1,0:T(8,128)(2,1)S(1)}, u32[]{:S(2)}, u32[]{:S(2)}) collective-permute-start(bf16[16,9216]{1,0:T(8,128)(2,1)S(1)} %pad_maximum_fusion.4), channel_id=1, source_target_pairs={{0,16},{1,17},{2,18},{3,19},{4,20},{5,21},{6,22},{7,23},{8,24},{9,... | collective-permute-start | bytes 884744 | tf_op jit(solution)/shard_map/ppermute | solution.py:61
  28.3 1.9 %copy-start.1 = (bf16[3072,512]{1,0:T(8,128)(2,1)S(1)}, bf16[3072,512]{1,0:T(8,128)(2,1)}, u32[]{:S(2)}) copy-start(bf16[3072,512]{1,0:T(8,128)(2,1)} %value_ref.3) | copy-start | bytes 9437188
  28.4 1.9 %copy-start.3 = (s32[24,512]{1,0:T(8,128)S(1)}, s32[24,512]{1,0:T(8,128)}, u32[]{:S(2)}) copy-start(s32[24,512]{1,0:T(8,128)} %mask_ref.3) | copy-start | bytes 147460
  28.4 7.8 %collective-permute-start.12 = (bf16[8,9216]{1,0:T(8,128)(2,1)S(1)}, bf16[8,9216]{1,0:T(8,128)(2,1)S(1)}, u32[]{:S(2)}, u32[]{:S(2)}) collective-permute-start(bf16[8,9216]{1,0:T(8,128)(2,1)S(1)} %get-tuple-element.36), channel_id=1, source_target_pairs={{0,16},{1,17},{2,18},{3,19},{4,20},{5,21},{6,22},{7,23},{8,24},{9,... | collective-permute-start | bytes 442376 | tf_op jit(solution)/shard_map/ppermute | solution.py:66
  30.5 12.9 %collective-permute-start.13 = (bf16[96,9216]{1,0:T(8,128)(2,1)S(1)}, bf16[96,9216]{1,0:T(8,128)(2,1)S(1)}, u32[]{:S(2)}, u32[]{:S(2)}) collective-permute-start(bf16[96,9216]{1,0:T(8,128)(2,1)S(1)} %get-tuple-element.15), channel_id=1, source_target_pairs={{0,1},{1,0},{2,3},{3,2},{4,5},{5,4},{6,7},{7,6},{8,9},{9,8},{10,11... | collective-permute-start | bytes 5308424 | tf_op jit(solution)/shard_map/ppermute | solution.py:297
  36.2 7.3 %collective-permute-start.14 = (bf16[32,9216]{1,0:T(8,128)(2,1)S(1)}, bf16[32,9216]{1,0:T(8,128)(2,1)S(1)}, u32[]{:S(2)}, u32[]{:S(2)}) collective-permute-start(bf16[32,9216]{1,0:T(8,128)(2,1)S(1)} %pad_maximum_fusion), channel_id=1, source_target_pairs={{0,1},{1,0},{2,3},{3,2},{4,5},{5,4},{6,7},{7,6},{8,9},{9,8},{10,11... | collective-permute-start | bytes 1769480 | tf_op jit(solution)/shard_map/ppermute | solution.py:298
  40.8 8.3 %collective-permute-start.16 = (f32[128,512]{1,0:T(8,128)S(1)}, f32[128,512]{1,0:T(8,128)S(1)}, u32[]{:S(2)}, u32[]{:S(2)}) collective-permute-start(f32[128,512]{1,0:T(8,128)S(1)} %rhs_mine.1), channel_id=1, source_target_pairs={{0,32},{1,97},{2,34},{3,99},{4,36},{5,101},{6,38},{7,103},{8,40},{... | collective-permute-start | bytes 786440 | tf_op jit(solution)/shard_map/ppermute | solution.py:290
  46.3 7.9 %collective-permute-start.17 = (f32[128,512]{1,0:T(8,128)S(1)}, f32[128,512]{1,0:T(8,128)S(1)}, u32[]{:S(2)}, u32[]{:S(2)}) collective-permute-start(f32[128,512]{1,0:T(8,128)S(1)} %rhs_other.1), channel_id=1, source_target_pairs={{0,32},{1,97},{2,34},{3,99},{4,36},{5,101},{6,38},{7,103},{8,40},{... | collective-permute-start | bytes 786440 | tf_op jit(solution)/shard_map/ppermute | solution.py:290
  46.6 7.6 %collective-permute-start.15 = (f32[128,256]{1,0:T(8,128)S(1)}, f32[128,256]{1,0:T(8,128)S(1)}, u32[]{:S(2)}, u32[]{:S(2)}) collective-permute-start(f32[128,256]{1,0:T(8,128)S(1)} %top_gram.1), channel_id=1, source_target_pairs={{0,32},{1,97},{2,34},{3,99},{4,36},{5,101},{6,38},{7,103},{8,40},{... | collective-permute-start | bytes 393224 | tf_op jit(solution)/shard_map/ppermute | solution.py:290
  54.3 14.5 %copy-start.4 = (s32[32]{0:T(128)S(1)}, s32[32]{0:T(128)}, u32[]{:S(2)}) copy-start(s32[32]{0:T(128)} %constant.73.clone) | copy-start | bytes 388
  54.3 14.5 %copy-start.5 = (s32[32]{0:T(128)S(1)}, s32[32]{0:T(128)}, u32[]{:S(2)}) copy-start(s32[32]{0:T(128)} %constant.74.clone) | copy-start | bytes 388
  54.4 8.5 %collective-permute-start.18 = (f32[256,512]{1,0:T(8,128)S(1)}, f32[256,512]{1,0:T(8,128)S(1)}, u32[]{:S(2)}, u32[]{:S(2)}) collective-permute-start(f32[256,512]{1,0:T(8,128)S(1)} %pad_maximum_fusion.1), channel_id=1, source_target_pairs={{0,96},{1,33},{2,98},{3,35},{4,100},{5,37},{6,102},{7,39},{8,104},... | collective-permute-start | bytes 1572872 | tf_op jit(solution)/shard_map/ppermute | solution.py:290
  54.5 5.4 %collective-permute-start.20 = (f32[128,256]{1,0:T(8,128)S(1)}, f32[128,256]{1,0:T(8,128)S(1)}, u32[]{:S(2)}, u32[]{:S(2)}) collective-permute-start(f32[128,256]{1,0:T(8,128)S(1)} %add.85), channel_id=1, source_target_pairs={{0,128},{1,129},{2,130},{3,131},{4,132},{5,133},{6,134},{7,135},{8... | collective-permute-start | bytes 393224 | tf_op jit(solution)/shard_map/ppermute | solution.py:290
  60.0 6.1 %collective-permute-start.21 = (f32[128,256]{1,0:T(8,128)S(1)}, f32[128,256]{1,0:T(8,128)S(1)}, u32[]{:S(2)}, u32[]{:S(2)}) collective-permute-start(f32[128,256]{1,0:T(8,128)S(1)} %add.86), channel_id=1, source_target_pairs={{0,96},{1,33},{2,98},{3,35},{4,100},{5,37},{6,102},{7,39},{8,104},... | collective-permute-start | bytes 393224 | tf_op jit(solution)/shard_map/ppermute | solution.py:290
  63.0 15.6 %collective-permute-start.19 = (f32[256,512]{1,0:T(8,128)S(1)}, f32[256,512]{1,0:T(8,128)S(1)}, u32[]{:S(2)}, u32[]{:S(2)}) collective-permute-start(f32[256,512]{1,0:T(8,128)S(1)} %fusion.7.rhs_ref), channel_id=1, source_target_pairs={{0,128},{1,129},{2,130},{3,131},{4,132},{5,133},{6,134},{7,135},{8... | collective-permute-start | bytes 1572872 | tf_op jit(solution)/shard_map/ppermute | solution.py:290
  66.1 3.6 %collective-permute-start.22 = (f32[128,256]{1,0:T(8,128)S(1)}, f32[128,256]{1,0:T(8,128)S(1)}, u32[]{:S(2)}, u32[]{:S(2)}) collective-permute-start(f32[128,256]{1,0:T(8,128)S(1)} %add.87.top_ref), channel_id=1, source_target_pairs={{0,1},{1,0},{2,3},{3,2},{4,5},{5,4},{6,7},{7,6},{8,9},{9,8},{10,11... | collective-permute-start | bytes 393224 | tf_op jit(solution)/shard_map/ppermute | solution.py:325

commit v4 on v3

--- a/solution.py
+++ b/solution.py
@@ -99,20 +99,35 @@
     return total + LAMBDA * tags
 
 
-def gram_kernel(users, mine_ref, other_ref, out_ref):
-    out_ref[:, :128] = weighted_gram(mine_ref, mine_ref, users)
+def own_kernel(users, mine_ref, out_ref):
+    out_ref[...] = weighted_gram(mine_ref, mine_ref, users)
+
+
+def gram_kernel(users, own_ref, mine_ref, other_ref, out_ref):
+    out_ref[:, :128] = own_ref[...]
     out_ref[:, 128:] = weighted_gram(mine_ref, other_ref, users)
 
 
-def top_gram(mine, other, n_users):
+def own_gram(mine, n_users):
+    return pl.pallas_call(
+        functools.partial(own_kernel, n_users),
+        out_shape=jax.ShapeDtypeStruct((128, 128), jnp.float32),
+        in_specs=[whole()],
+        out_specs=whole(),
+        compiler_params=pltpu.CompilerParams(vmem_limit_bytes=4 << 20),
+        name="own_gram",
+    )(mine)
+
+
+def top_gram(own, mine, other, n_users):
     return pl.pallas_call(
         functools.partial(gram_kernel, n_users),
         out_shape=jax.ShapeDtypeStruct((128, 256), jnp.float32),
-        in_specs=[whole(), whole()],
+        in_specs=[whole()] * 3,
         out_specs=whole(),
         compiler_params=pltpu.CompilerParams(vmem_limit_bytes=4 << 20),
         name="top_gram",
-    )(mine, other)
+    )(own, mine, other)
 
 
 def rhs_kernel(factor_ref, *refs):
@@ -312,7 +327,7 @@
     order = (((y + dy) % NY) * NZ + (z + dz) % NZ) * NC + (c + dc) % NC
 
     rhs_mine = rhs_rows(mine, parts, "rhs_mine")
-    top = top_gram(mine, other, n_users)
+    top = top_gram(own_gram(mine, n_users), mine, other, n_users)
     top, later = lax.optimization_barrier((top, other))
     rhs_other = rhs_rows(later, parts, "rhs_other")
 

time: 80.1 us -> 80.3 us (level)
  no operation moved by 1% of the time
where the time goes in v4:
time: 80.3 us; the launch traced here: 80.2 us
  starting transfers between devices  46 us (57%)
  waiting for transfers between devices  16.8 us (21%)
  Pallas kernels  15.2 us (19%)
  other arithmetic  1.32 us (2%)
    ppermute x7, starting transfers between devices, swap(): return lax.ppermute(value, ('band', 'item'), band_perm(stage))  14.4 us
    pallas_call x1, Pallas kernels, ordered_inverse(): pl.pallas_call(inverse_kernel, out_shape=jax.ShapeDtypeStruct((n, n), jnp...  8.83 us
    ppermute x7, waiting for transfers between devices, swap(): return lax.ppermute(value, ('band', 'item'), band_perm(stage))  7.57 us
    ppermute x3, starting transfers between devices, gather_columns(): down = lax.ppermute(down, 'item', DOWN)  7.55 us
    ppermute x3, waiting for transfers between devices, gather_columns(): up = lax.ppermute(up, 'item', UP)  7.12 us
    ppermute x1, starting transfers between devices, body(): other_first = lax.ppermute(first, 'item', CORE)  5.69 us
    ppermute x3, starting transfers between devices, gather_columns(): up = lax.ppermute(up, 'item', UP)  4.38 us
    ppermute x4, starting transfers between devices, gather_columns(): far.append(lax.ppermute(pending, 'item', ACROSS))  4.32 us
  transfers between devices with their start and end apart: 23, of which 8 were waited for; matrix products, arithmetic and copies ran while one was open for 1% of the time, Pallas kernels for 17%

profile of v4, /device:TPU:1, one launch (start us, length us, event | category | flops | bytes accessed | tf_op | source)
XLA Modules:
  0.0 80.2 jit_solution(10201493589202221515)
XLA Ops:
  0.0 1.0 %constant_dynamic-update-slice_fusion.24 = (bf16[96,9216]{1,0:T(8,128)(2,1)S(1)}, bf16[128,9216]{1,0:T(8,128)(2,1)S(1)}, bf16[8,9216]{1,0:T(8,128)(2,1)S(1)}) fusion(bf16[8,3072]{1,0:T(8,128)(2,1)} %bitcast.3, bf16[8,6144]{1,0:T(8,128)(2,1)} %bitcast.2), kind=kLoop, calls=%fused_computation.30 | loop fusion | flops 294910 | bytes 589824
  1.0 2.5 %collective-permute-start = (bf16[8,9216]{1,0:T(8,128)(2,1)S(1)}, bf16[8,9216]{1,0:T(8,128)(2,1)S(1)}, u32[]{:S(2)}, u32[]{:S(2)}) collective-permute-start(bf16[8,9216]{1,0:T(8,128)(2,1)S(1)} %get-tuple-element.35), channel_id=1, source_target_pairs={{0,2},{1,3},{2,4},{3,5},{4,6},{5,7},{6,8},{7,9},{8,10},{9,11},{10,... | collective-permute-start | bytes 442376 | tf_op jit(solution)/shard_map/ppermute | solution.py:58
  3.5 4.0 %collective-permute-start.1 = (bf16[8,9216]{1,0:T(8,128)(2,1)S(1)}, bf16[8,9216]{1,0:T(8,128)(2,1)S(1)}, u32[]{:S(2)}, u32[]{:S(2)}) collective-permute-start(bf16[8,9216]{1,0:T(8,128)(2,1)S(1)} %get-tuple-element.35), channel_id=1, source_target_pairs={{0,14},{1,15},{2,0},{3,1},{4,2},{5,3},{6,4},{7,5},{8,6},{9,7},{10,... | collective-permute-start | bytes 442376 | tf_op jit(solution)/shard_map/ppermute | solution.py:57
  7.5 1.3 %collective-permute-start.6 = (bf16[8,9216]{1,0:T(8,128)(2,1)S(1)}, bf16[8,9216]{1,0:T(8,128)(2,1)S(1)}, u32[]{:S(2)}, u32[]{:S(2)}) collective-permute-start(bf16[8,9216]{1,0:T(8,128)(2,1)S(1)} %get-tuple-element.35), channel_id=1, source_target_pairs={{0,16},{1,17},{2,18},{3,19},{4,20},{5,21},{6,22},{7,23},{8,24},{9,... | collective-permute-start | bytes 442376 | tf_op jit(solution)/shard_map/ppermute | solution.py:56
  8.8 2.2 %collective-permute-done = bf16[8,9216]{1,0:T(8,128)(2,1)S(1)} collective-permute-done((bf16[8,9216]{1,0:T(8,128)(2,1)S(1)}, bf16[8,9216]{1,0:T(8,128)(2,1)S(1)}, u32[]{:S(2)}, u32[]{:S(2)}) %collective-permute-start) | collective-permute-done | bytes 147488 | tf_op jit(solution)/shard_map/ppermute | solution.py:58
  11.0 1.4 %collective-permute-start.7 = (bf16[16,9216]{1,0:T(8,128)(2,1)S(1)}, bf16[16,9216]{1,0:T(8,128)(2,1)S(1)}, u32[]{:S(2)}, u32[]{:S(2)}) collective-permute-start(bf16[16,9216]{1,0:T(8,128)(2,1)S(1)} %pad_maximum_fusion.2), channel_id=1, source_target_pairs={{0,16},{1,17},{2,18},{3,19},{4,20},{5,21},{6,22},{7,23},{8,24},{9,... | collective-permute-start | bytes 884744 | tf_op jit(solution)/shard_map/ppermute | solution.py:56
  12.4 2.7 %collective-permute-start.3 = (bf16[8,9216]{1,0:T(8,128)(2,1)S(1)}, bf16[8,9216]{1,0:T(8,128)(2,1)S(1)}, u32[]{:S(2)}, u32[]{:S(2)}) collective-permute-start(bf16[8,9216]{1,0:T(8,128)(2,1)S(1)} %collective-permute-done.1), channel_id=1, source_target_pairs={{0,14},{1,15},{2,0},{3,1},{4,2},{5,3},{6,4},{7,5},{8,6},{9,7},{10,... | collective-permute-start | bytes 442376 | tf_op jit(solution)/shard_map/ppermute | solution.py:57
  15.2 2.5 %collective-permute-done.2 = bf16[8,9216]{1,0:T(8,128)(2,1)S(1)} collective-permute-done((bf16[8,9216]{1,0:T(8,128)(2,1)S(1)}, bf16[8,9216]{1,0:T(8,128)(2,1)S(1)}, u32[]{:S(2)}, u32[]{:S(2)}) %collective-permute-start.2) | collective-permute-done | bytes 147488 | tf_op jit(solution)/shard_map/ppermute | solution.py:58
  17.7 0.3 collective-permute-start.8
  17.9 1.8 %collective-permute-start.4 = (bf16[8,9216]{1,0:T(8,128)(2,1)S(1)}, bf16[8,9216]{1,0:T(8,128)(2,1)S(1)}, u32[]{:S(2)}, u32[]{:S(2)}) collective-permute-start(bf16[8,9216]{1,0:T(8,128)(2,1)S(1)} %collective-permute-done.2), channel_id=1, source_target_pairs={{0,2},{1,3},{2,4},{3,5},{4,6},{5,7},{6,8},{7,9},{8,10},{9,11},{10,... | collective-permute-start | bytes 442376 | tf_op jit(solution)/shard_map/ppermute | solution.py:58
  19.7 0.8 %collective-permute-start.5 = (bf16[8,9216]{1,0:T(8,128)(2,1)S(1)}, bf16[8,9216]{1,0:T(8,128)(2,1)S(1)}, u32[]{:S(2)}, u32[]{:S(2)}) collective-permute-start(bf16[8,9216]{1,0:T(8,128)(2,1)S(1)} %collective-permute-done.3), channel_id=1, source_target_pairs={{0,14},{1,15},{2,0},{3,1},{4,2},{5,3},{6,4},{7,5},{8,6},{9,7},{10,... | collective-permute-start | bytes 442376 | tf_op jit(solution)/shard_map/ppermute | solution.py:57
  20.6 2.5 %collective-permute-done.4 = bf16[8,9216]{1,0:T(8,128)(2,1)S(1)} collective-permute-done((bf16[8,9216]{1,0:T(8,128)(2,1)S(1)}, bf16[8,9216]{1,0:T(8,128)(2,1)S(1)}, u32[]{:S(2)}, u32[]{:S(2)}) %collective-permute-start.4) | collective-permute-done | bytes 147488 | tf_op jit(solution)/shard_map/ppermute | solution.py:58
  23.1 0.6 collective-permute-start.9
  23.7 0.3 collective-permute-done.5
  24.0 1.8 %collective-permute-start.10 = (bf16[8,4608]{1,0:T(8,128)(2,1)S(1)}, bf16[8,4608]{1,0:T(8,128)(2,1)S(1)}, u32[]{:S(2)}, u32[]{:S(2)}) collective-permute-start(bf16[8,4608]{1,0:T(8,128)(2,1)S(1)} %slice.9), channel_id=1, source_target_pairs={{0,14},{1,15},{2,0},{3,1},{4,2},{5,3},{6,4},{7,5},{8,6},{9,7},{10,... | collective-permute-start | bytes 221192 | tf_op jit(solution)/shard_map/ppermute | solution.py:63
  26.0 1.4 %collective-permute-start.11 = (bf16[16,9216]{1,0:T(8,128)(2,1)S(1)}, bf16[16,9216]{1,0:T(8,128)(2,1)S(1)}, u32[]{:S(2)}, u32[]{:S(2)}) collective-permute-start(bf16[16,9216]{1,0:T(8,128)(2,1)S(1)} %pad_maximum_fusion.4), channel_id=1, source_target_pairs={{0,16},{1,17},{2,18},{3,19},{4,20},{5,21},{6,22},{7,23},{8,24},{9,... | collective-permute-start | bytes 884744 | tf_op jit(solution)/shard_map/ppermute | solution.py:61
  27.5 0.0 collective-permute-done.9
  27.6 0.8 collective-permute-done.10
  28.3 0.0 copy-start.1
  28.4 0.0 copy-start.3
  28.4 1.4 %collective-permute-start.12 = (bf16[8,9216]{1,0:T(8,128)(2,1)S(1)}, bf16[8,9216]{1,0:T(8,128)(2,1)S(1)}, u32[]{:S(2)}, u32[]{:S(2)}) collective-permute-start(bf16[8,9216]{1,0:T(8,128)(2,1)S(1)} %get-tuple-element.36), channel_id=1, source_target_pairs={{0,16},{1,17},{2,18},{3,19},{4,20},{5,21},{6,22},{7,23},{8,24},{9,... | collective-permute-start | bytes 442376 | tf_op jit(solution)/shard_map/ppermute | solution.py:66
  29.8 0.4 mask_users.1.refs_0_
  30.2 0.0 copy-done.1
  30.2 0.2 mask_tags.1.refs_1_
  30.5 5.7 %collective-permute-start.13 = (bf16[96,9216]{1,0:T(8,128)(2,1)S(1)}, bf16[96,9216]{1,0:T(8,128)(2,1)S(1)}, u32[]{:S(2)}, u32[]{:S(2)}) collective-permute-start(bf16[96,9216]{1,0:T(8,128)(2,1)S(1)} %get-tuple-element.15), channel_id=1, source_target_pairs={{0,1},{1,0},{2,3},{3,2},{4,5},{5,4},{6,7},{7,6},{8,9},{9,8},{10,11... | collective-permute-start | bytes 5308424 | tf_op jit(solution)/shard_map/ppermute | solution.py:312
  36.2 3.1 %collective-permute-start.14 = (bf16[32,9216]{1,0:T(8,128)(2,1)S(1)}, bf16[32,9216]{1,0:T(8,128)(2,1)S(1)}, u32[]{:S(2)}, u32[]{:S(2)}) collective-permute-start(bf16[32,9216]{1,0:T(8,128)(2,1)S(1)} %pad_maximum_fusion), channel_id=1, source_target_pairs={{0,1},{1,0},{2,3},{3,2},{4,5},{5,4},{6,7},{7,6},{8,9},{9,8},{10,11... | collective-permute-start | bytes 1769480 | tf_op jit(solution)/shard_map/ppermute | solution.py:313
  39.4 0.8 own_gram.1.own_ref
  40.2 1.4 %rhs_mine.1 = f32[128,512]{1,0:T(8,128)S(1)} custom-call(bf16[128,9216]{1,0:T(8,128)(2,1)S(1)} %constant_dynamic-update-slice_fusion.2.factor_ref.mine_ref, bf16[6144,512]{1,0:T(8,128)(2,1)S(1)} %mask_users.1.refs_0_, bf16[3072,512]{1,0:T(8,128)(2,1)S(1)} %mask_tags.1.refs_1_), custom_call_target="tpu_custom_call" | custom-call | tf_op jit(solution)/shard_map/rhs_mine/pallas_call | solution.py:146
  41.6 2.6 %collective-permute-start.16 = (f32[128,512]{1,0:T(8,128)S(1)}, f32[128,512]{1,0:T(8,128)S(1)}, u32[]{:S(2)}, u32[]{:S(2)}) collective-permute-start(f32[128,512]{1,0:T(8,128)S(1)} %rhs_mine.1), channel_id=1, source_target_pairs={{0,32},{1,97},{2,34},{3,99},{4,36},{5,101},{6,38},{7,103},{8,40},{... | collective-permute-start | bytes 786440 | tf_op jit(solution)/shard_map/ppermute | solution.py:305
  44.1 0.1 constant_dynamic-update-slice_fusion.26
  44.3 0.8 top_gram.1
  45.1 1.4 %rhs_other.1 = f32[128,512]{1,0:T(8,128)S(1)} custom-call(bf16[128,9216]{1,0:T(8,128)(2,1)S(1)} %constant_dynamic-update-slice_fusion.25.other_ref.factor_ref, bf16[6144,512]{1,0:T(8,128)(2,1)S(1)} %mask_users.1.refs_0_, bf16[3072,512]{1,0:T(8,128)(2,1)S(1)} %mask_tags.1.refs_1_), custom_call_target="tpu_custom_call" | custom-call | tf_op jit(solution)/shard_map/rhs_other/pallas_call | solution.py:146
  46.5 0.3 collective-permute-start.17
  46.8 2.5 %collective-permute-start.15 = (f32[128,256]{1,0:T(8,128)S(1)}, f32[128,256]{1,0:T(8,128)S(1)}, u32[]{:S(2)}, u32[]{:S(2)}) collective-permute-start(f32[128,256]{1,0:T(8,128)S(1)} %top_gram.1), channel_id=1, source_target_pairs={{0,32},{1,97},{2,34},{3,99},{4,36},{5,101},{6,38},{7,103},{8,40},{... | collective-permute-start | bytes 393224 | tf_op jit(solution)/shard_map/ppermute | solution.py:305
  49.2 5.2 %collective-permute-done.15 = f32[128,256]{1,0:T(8,128)S(1)} collective-permute-done((f32[128,256]{1,0:T(8,128)S(1)}, f32[128,256]{1,0:T(8,128)S(1)}, u32[]{:S(2)}, u32[]{:S(2)}) %collective-permute-start.15) | collective-permute-done | bytes 131104 | tf_op jit(solution)/shard_map/ppermute | solution.py:305
  54.4 0.0 copy-start.4
  54.4 0.0 copy-start.5
  54.6 0.1 collective-permute-start.18
  54.7 3.0 %collective-permute-start.20 = (f32[128,256]{1,0:T(8,128)S(1)}, f32[128,256]{1,0:T(8,128)S(1)}, u32[]{:S(2)}, u32[]{:S(2)}) collective-permute-start(f32[128,256]{1,0:T(8,128)S(1)} %add.85), channel_id=1, source_target_pairs={{0,128},{1,129},{2,130},{3,131},{4,132},{5,133},{6,134},{7,135},{8... | collective-permute-start | bytes 393224 | tf_op jit(solution)/shard_map/ppermute | solution.py:305
  57.7 2.4 %collective-permute-done.20 = f32[128,256]{1,0:T(8,128)S(1)} collective-permute-done((f32[128,256]{1,0:T(8,128)S(1)}, f32[128,256]{1,0:T(8,128)S(1)}, u32[]{:S(2)}, u32[]{:S(2)}) %collective-permute-start.20) | collective-permute-done | bytes 131104 | tf_op jit(solution)/shard_map/ppermute | solution.py:305
  60.1 2.9 %collective-permute-start.21 = (f32[128,256]{1,0:T(8,128)S(1)}, f32[128,256]{1,0:T(8,128)S(1)}, u32[]{:S(2)}, u32[]{:S(2)}) collective-permute-start(f32[128,256]{1,0:T(8,128)S(1)} %add.86), channel_id=1, source_target_pairs={{0,96},{1,33},{2,98},{3,35},{4,100},{5,37},{6,102},{7,39},{8,104},... | collective-permute-start | bytes 393224 | tf_op jit(solution)/shard_map/ppermute | solution.py:305
  63.0 0.1 fusion.7.rhs_ref
  63.1 3.0 %collective-permute-start.19 = (f32[256,512]{1,0:T(8,128)S(1)}, f32[256,512]{1,0:T(8,128)S(1)}, u32[]{:S(2)}, u32[]{:S(2)}) collective-permute-start(f32[256,512]{1,0:T(8,128)S(1)} %fusion.7.rhs_ref), channel_id=1, source_target_pairs={{0,128},{1,129},{2,130},{3,131},{4,132},{5,133},{6,134},{7,135},{8... | collective-permute-start | bytes 1572872 | tf_op jit(solution)/shard_map/ppermute | solution.py:305
  66.1 0.1 add.82
  66.3 2.7 %collective-permute-start.22 = (f32[128,256]{1,0:T(8,128)S(1)}, f32[128,256]{1,0:T(8,128)S(1)}, u32[]{:S(2)}, u32[]{:S(2)}) collective-permute-start(f32[128,256]{1,0:T(8,128)S(1)} %add.87.top_ref), channel_id=1, source_target_pairs={{0,1},{1,0},{2,3},{3,2},{4,5},{5,4},{6,7},{7,6},{8,9},{9,8},{10,11... | collective-permute-start | bytes 393224 | tf_op jit(solution)/shard_map/ppermute | solution.py:340
  68.9 1.0 %collective-permute-done.22.peer_ref = f32[128,256]{1,0:T(8,128)S(1)} collective-permute-done((f32[128,256]{1,0:T(8,128)S(1)}, f32[128,256]{1,0:T(8,128)S(1)}, u32[]{:S(2)}, u32[]{:S(2)}) %collective-permute-start.22) | collective-permute-done | bytes 131104 | tf_op jit(solution)/shard_map/ppermute | solution.py:340
  69.9 8.8 %ordered_inverse.1.inverse_ref = f32[256,256]{1,0:T(8,128)S(1)} custom-call(s32[32]{0:T(128)S(1)} %fusion.1.order_ref, f32[128,256]{1,0:T(8,128)S(1)} %add.87.top_ref, f32[128,256]{1,0:T(8,128)S(1)} %collective-permute-done.22.peer_ref), custom_call_target="tpu_custom_call" | custom-call | flops 2000000000 | tf_op jit(solution)/shard_map/ordered_inverse/pallas_call | solution.py:270
  78.8 1.4 %final_solve.1 = f32[512,256]{1,0:T(8,128)} custom-call(f32[256,512]{1,0:T(8,128)S(1)} %fusion.7.rhs_ref, f32[256,512]{1,0:T(8,128)S(1)} %collective-permute-done.19.more_ref, f32[256,256]{1,0:T(8,128)S(1)} %ordered_inverse.1.inverse_ref), custom_call_target="tpu_custom_call" | custom-call | tf_op jit(solution)/shard_map/final_solve/pallas_call | solution.py:294
  (50 shorter events, 0.7 us)
Async XLA Ops:
  1.0 10.1 %collective-permute-start = (bf16[8,9216]{1,0:T(8,128)(2,1)S(1)}, bf16[8,9216]{1,0:T(8,128)(2,1)S(1)}, u32[]{:S(2)}, u32[]{:S(2)}) collective-permute-start(bf16[8,9216]{1,0:T(8,128)(2,1)S(1)} %get-tuple-element.35), channel_id=1, source_target_pairs={{0,2},{1,3},{2,4},{3,5},{4,6},{5,7},{6,8},{7,9},{8,10},{9,11},{10,... | collective-permute-start | bytes 442376 | tf_op jit(solution)/shard_map/ppermute | solution.py:58
  3.5 7.5 %collective-permute-start.1 = (bf16[8,9216]{1,0:T(8,128)(2,1)S(1)}, bf16[8,9216]{1,0:T(8,128)(2,1)S(1)}, u32[]{:S(2)}, u32[]{:S(2)}) collective-permute-start(bf16[8,9216]{1,0:T(8,128)(2,1)S(1)} %get-tuple-element.35), channel_id=1, source_target_pairs={{0,14},{1,15},{2,0},{3,1},{4,2},{5,3},{6,4},{7,5},{8,6},{9,7},{10,... | collective-permute-start | bytes 442376 | tf_op jit(solution)/shard_map/ppermute | solution.py:57
  7.5 18.4 %collective-permute-start.6 = (bf16[8,9216]{1,0:T(8,128)(2,1)S(1)}, bf16[8,9216]{1,0:T(8,128)(2,1)S(1)}, u32[]{:S(2)}, u32[]{:S(2)}) collective-permute-start(bf16[8,9216]{1,0:T(8,128)(2,1)S(1)} %get-tuple-element.35), channel_id=1, source_target_pairs={{0,16},{1,17},{2,18},{3,19},{4,20},{5,21},{6,22},{7,23},{8,24},{9,... | collective-permute-start | bytes 442376 | tf_op jit(solution)/shard_map/ppermute | solution.py:56
  11.0 16.4 %collective-permute-start.7 = (bf16[16,9216]{1,0:T(8,128)(2,1)S(1)}, bf16[16,9216]{1,0:T(8,128)(2,1)S(1)}, u32[]{:S(2)}, u32[]{:S(2)}) collective-permute-start(bf16[16,9216]{1,0:T(8,128)(2,1)S(1)} %pad_maximum_fusion.2), channel_id=1, source_target_pairs={{0,16},{1,17},{2,18},{3,19},{4,20},{5,21},{6,22},{7,23},{8,24},{9,... | collective-permute-start | bytes 884744 | tf_op jit(solution)/shard_map/ppermute | solution.py:56
  12.4 5.2 %collective-permute-start.2 = (bf16[8,9216]{1,0:T(8,128)(2,1)S(1)}, bf16[8,9216]{1,0:T(8,128)(2,1)S(1)}, u32[]{:S(2)}, u32[]{:S(2)}) collective-permute-start(bf16[8,9216]{1,0:T(8,128)(2,1)S(1)} %collective-permute-done), channel_id=1, source_target_pairs={{0,2},{1,3},{2,4},{3,5},{4,6},{5,7},{6,8},{7,9},{8,10},{9,11},{10,... | collective-permute-start | bytes 442376 | tf_op jit(solution)/shard_map/ppermute | solution.py:58
  12.4 5.2 %collective-permute-start.3 = (bf16[8,9216]{1,0:T(8,128)(2,1)S(1)}, bf16[8,9216]{1,0:T(8,128)(2,1)S(1)}, u32[]{:S(2)}, u32[]{:S(2)}) collective-permute-start(bf16[8,9216]{1,0:T(8,128)(2,1)S(1)} %collective-permute-done.1), channel_id=1, source_target_pairs={{0,14},{1,15},{2,0},{3,1},{4,2},{5,3},{6,4},{7,5},{8,6},{9,7},{10,... | collective-permute-start | bytes 442376 | tf_op jit(solution)/shard_map/ppermute | solution.py:57
  15.1 14.7 %copy-start.2 = (s32[48,512]{1,0:T(8,128)S(1)}, s32[48,512]{1,0:T(8,128)}, u32[]{:S(2)}) copy-start(s32[48,512]{1,0:T(8,128)} %mask_ref.2) | copy-start | bytes 294916
  15.1 14.6 %copy-start = (bf16[6144,512]{1,0:T(8,128)(2,1)S(1)}, bf16[6144,512]{1,0:T(8,128)(2,1)}, u32[]{:S(2)}) copy-start(bf16[6144,512]{1,0:T(8,128)(2,1)} %value_ref.2) | copy-start | bytes 18874372
  17.7 9.8 %collective-permute-start.8 = (bf16[16,9216]{1,0:T(8,128)(2,1)S(1)}, bf16[16,9216]{1,0:T(8,128)(2,1)S(1)}, u32[]{:S(2)}, u32[]{:S(2)}) collective-permute-start(bf16[16,9216]{1,0:T(8,128)(2,1)S(1)} %pad_maximum_fusion.3), channel_id=1, source_target_pairs={{0,16},{1,17},{2,18},{3,19},{4,20},{5,21},{6,22},{7,23},{8,24},{9,... | collective-permute-start | bytes 884744 | tf_op jit(solution)/shard_map/ppermute | solution.py:56
  17.9 5.2 %collective-permute-start.4 = (bf16[8,9216]{1,0:T(8,128)(2,1)S(1)}, bf16[8,9216]{1,0:T(8,128)(2,1)S(1)}, u32[]{:S(2)}, u32[]{:S(2)}) collective-permute-start(bf16[8,9216]{1,0:T(8,128)(2,1)S(1)} %collective-permute-done.2), channel_id=1, source_target_pairs={{0,2},{1,3},{2,4},{3,5},{4,6},{5,7},{6,8},{7,9},{8,10},{9,11},{10,... | collective-permute-start | bytes 442376 | tf_op jit(solution)/shard_map/ppermute | solution.py:58
  19.7 4.3 %collective-permute-start.5 = (bf16[8,9216]{1,0:T(8,128)(2,1)S(1)}, bf16[8,9216]{1,0:T(8,128)(2,1)S(1)}, u32[]{:S(2)}, u32[]{:S(2)}) collective-permute-start(bf16[8,9216]{1,0:T(8,128)(2,1)S(1)} %collective-permute-done.3), channel_id=1, source_target_pairs={{0,14},{1,15},{2,0},{3,1},{4,2},{5,3},{6,4},{7,5},{8,6},{9,7},{10,... | collective-permute-start | bytes 442376 | tf_op jit(solution)/shard_map/ppermute | solution.py:57
  23.1 4.4 %collective-permute-start.9 = (bf16[8,4608]{1,0:T(8,128)(2,1)S(1)}, bf16[8,4608]{1,0:T(8,128)(2,1)S(1)}, u32[]{:S(2)}, u32[]{:S(2)}) collective-permute-start(bf16[8,4608]{1,0:T(8,128)(2,1)S(1)} %slice.8), channel_id=1, source_target_pairs={{0,2},{1,3},{2,4},{3,5},{4,6},{5,7},{6,8},{7,9},{8,10},{9,11},{10,... | collective-permute-start | bytes 221192 | tf_op jit(solution)/shard_map/ppermute | solution.py:63
  24.0 4.3 %collective-permute-start.10 = (bf16[8,4608]{1,0:T(8,128)(2,1)S(1)}, bf16[8,4608]{1,0:T(8,128)(2,1)S(1)}, u32[]{:S(2)}, u32[]{:S(2)}) collective-permute-start(bf16[8,4608]{1,0:T(8,128)(2,1)S(1)} %slice.9), channel_id=1, source_target_pairs={{0,14},{1,15},{2,0},{3,1},{4,2},{5,3},{6,4},{7,5},{8,6},{9,7},{10,... | collective-permute-start | bytes 221192 | tf_op jit(solution)/shard_map/ppermute | solution.py:63
  26.0 10.2 %collective-permute-start.11 = (bf16[16,9216]{1,0:T(8,128)(2,1)S(1)}, bf16[16,9216]{1,0:T(8,128)(2,1)S(1)}, u32[]{:S(2)}, u32[]{:S(2)}) collective-permute-start(bf16[16,9216]{1,0:T(8,128)(2,1)S(1)} %pad_maximum_fusion.4), channel_id=1, source_target_pairs={{0,16},{1,17},{2,18},{3,19},{4,20},{5,21},{6,22},{7,23},{8,24},{9,... | collective-permute-start | bytes 884744 | tf_op jit(solution)/shard_map/ppermute | solution.py:61
  28.3 1.9 %copy-start.1 = (bf16[3072,512]{1,0:T(8,128)(2,1)S(1)}, bf16[3072,512]{1,0:T(8,128)(2,1)}, u32[]{:S(2)}) copy-start(bf16[3072,512]{1,0:T(8,128)(2,1)} %value_ref.3) | copy-start | bytes 9437188
  28.4 1.9 %copy-start.3 = (s32[24,512]{1,0:T(8,128)S(1)}, s32[24,512]{1,0:T(8,128)}, u32[]{:S(2)}) copy-start(s32[24,512]{1,0:T(8,128)} %mask_ref.3) | copy-start | bytes 147460
  28.4 7.8 %collective-permute-start.12 = (bf16[8,9216]{1,0:T(8,128)(2,1)S(1)}, bf16[8,9216]{1,0:T(8,128)(2,1)S(1)}, u32[]{:S(2)}, u32[]{:S(2)}) collective-permute-start(bf16[8,9216]{1,0:T(8,128)(2,1)S(1)} %get-tuple-element.36), channel_id=1, source_target_pairs={{0,16},{1,17},{2,18},{3,19},{4,20},{5,21},{6,22},{7,23},{8,24},{9,... | collective-permute-start | bytes 442376 | tf_op jit(solution)/shard_map/ppermute | solution.py:66
  30.5 13.7 %collective-permute-start.13 = (bf16[96,9216]{1,0:T(8,128)(2,1)S(1)}, bf16[96,9216]{1,0:T(8,128)(2,1)S(1)}, u32[]{:S(2)}, u32[]{:S(2)}) collective-permute-start(bf16[96,9216]{1,0:T(8,128)(2,1)S(1)} %get-tuple-element.15), channel_id=1, source_target_pairs={{0,1},{1,0},{2,3},{3,2},{4,5},{5,4},{6,7},{7,6},{8,9},{9,8},{10,11... | collective-permute-start | bytes 5308424 | tf_op jit(solution)/shard_map/ppermute | solution.py:312
  36.2 8.0 %collective-permute-start.14 = (bf16[32,9216]{1,0:T(8,128)(2,1)S(1)}, bf16[32,9216]{1,0:T(8,128)(2,1)S(1)}, u32[]{:S(2)}, u32[]{:S(2)}) collective-permute-start(bf16[32,9216]{1,0:T(8,128)(2,1)S(1)} %pad_maximum_fusion), channel_id=1, source_target_pairs={{0,1},{1,0},{2,3},{3,2},{4,5},{5,4},{6,7},{7,6},{8,9},{9,8},{10,11... | collective-permute-start | bytes 1769480 | tf_op jit(solution)/shard_map/ppermute | solution.py:313
  41.6 7.7 %collective-permute-start.16 = (f32[128,512]{1,0:T(8,128)S(1)}, f32[128,512]{1,0:T(8,128)S(1)}, u32[]{:S(2)}, u32[]{:S(2)}) collective-permute-start(f32[128,512]{1,0:T(8,128)S(1)} %rhs_mine.1), channel_id=1, source_target_pairs={{0,32},{1,97},{2,34},{3,99},{4,36},{5,101},{6,38},{7,103},{8,40},{... | collective-permute-start | bytes 786440 | tf_op jit(solution)/shard_map/ppermute | solution.py:305
  46.5 7.9 %collective-permute-start.17 = (f32[128,512]{1,0:T(8,128)S(1)}, f32[128,512]{1,0:T(8,128)S(1)}, u32[]{:S(2)}, u32[]{:S(2)}) collective-permute-start(f32[128,512]{1,0:T(8,128)S(1)} %rhs_other.1), channel_id=1, source_target_pairs={{0,32},{1,97},{2,34},{3,99},{4,36},{5,101},{6,38},{7,103},{8,40},{... | collective-permute-start | bytes 786440 | tf_op jit(solution)/shard_map/ppermute | solution.py:305
  46.8 7.6 %collective-permute-start.15 = (f32[128,256]{1,0:T(8,128)S(1)}, f32[128,256]{1,0:T(8,128)S(1)}, u32[]{:S(2)}, u32[]{:S(2)}) collective-permute-start(f32[128,256]{1,0:T(8,128)S(1)} %top_gram.1), channel_id=1, source_target_pairs={{0,32},{1,97},{2,34},{3,99},{4,36},{5,101},{6,38},{7,103},{8,40},{... | collective-permute-start | bytes 393224 | tf_op jit(solution)/shard_map/ppermute | solution.py:305
  54.4 14.5 %copy-start.4 = (s32[32]{0:T(128)S(1)}, s32[32]{0:T(128)}, u32[]{:S(2)}) copy-start(s32[32]{0:T(128)} %constant.73.clone) | copy-start | bytes 388
  54.4 14.5 %copy-start.5 = (s32[32]{0:T(128)S(1)}, s32[32]{0:T(128)}, u32[]{:S(2)}) copy-start(s32[32]{0:T(128)} %constant.74.clone) | copy-start | bytes 388
  54.6 8.5 %collective-permute-start.18 = (f32[256,512]{1,0:T(8,128)S(1)}, f32[256,512]{1,0:T(8,128)S(1)}, u32[]{:S(2)}, u32[]{:S(2)}) collective-permute-start(f32[256,512]{1,0:T(8,128)S(1)} %pad_maximum_fusion.1), channel_id=1, source_target_pairs={{0,96},{1,33},{2,98},{3,35},{4,100},{5,37},{6,102},{7,39},{8,104},... | collective-permute-start | bytes 1572872 | tf_op jit(solution)/shard_map/ppermute | solution.py:305
  54.7 5.4 %collective-permute-start.20 = (f32[128,256]{1,0:T(8,128)S(1)}, f32[128,256]{1,0:T(8,128)S(1)}, u32[]{:S(2)}, u32[]{:S(2)}) collective-permute-start(f32[128,256]{1,0:T(8,128)S(1)} %add.85), channel_id=1, source_target_pairs={{0,128},{1,129},{2,130},{3,131},{4,132},{5,133},{6,134},{7,135},{8... | collective-permute-start | bytes 393224 | tf_op jit(solution)/shard_map/ppermute | solution.py:305
  60.1 6.1 %collective-permute-start.21 = (f32[128,256]{1,0:T(8,128)S(1)}, f32[128,256]{1,0:T(8,128)S(1)}, u32[]{:S(2)}, u32[]{:S(2)}) collective-permute-start(f32[128,256]{1,0:T(8,128)S(1)} %add.86), channel_id=1, source_target_pairs={{0,96},{1,33},{2,98},{3,35},{4,100},{5,37},{6,102},{7,39},{8,104},... | collective-permute-start | bytes 393224 | tf_op jit(solution)/shard_map/ppermute | solution.py:305
  63.1 15.6 %collective-permute-start.19 = (f32[256,512]{1,0:T(8,128)S(1)}, f32[256,512]{1,0:T(8,128)S(1)}, u32[]{:S(2)}, u32[]{:S(2)}) collective-permute-start(f32[256,512]{1,0:T(8,128)S(1)} %fusion.7.rhs_ref), channel_id=1, source_target_pairs={{0,128},{1,129},{2,130},{3,131},{4,132},{5,133},{6,134},{7,135},{8... | collective-permute-start | bytes 1572872 | tf_op jit(solution)/shard_map/ppermute | solution.py:305
  66.3 3.6 %collective-permute-start.22 = (f32[128,256]{1,0:T(8,128)S(1)}, f32[128,256]{1,0:T(8,128)S(1)}, u32[]{:S(2)}, u32[]{:S(2)}) collective-permute-start(f32[128,256]{1,0:T(8,128)S(1)} %add.87.top_ref), channel_id=1, source_target_pairs={{0,1},{1,0},{2,3},{3,2},{4,5},{5,4},{6,7},{7,6},{8,9},{9,8},{10,11... | collective-permute-start | bytes 393224 | tf_op jit(solution)/shard_map/ppermute | solution.py:340
